TPU v7x, 32 devices: a whole 2x2x4 slice. The times are simulated.
32 devices in a mesh: section: 2 (over core), stream: 4 (over y, x), slab: 4 (over z).
Axes of the slice: x: 2, y: 2, z: 4, core: 2. Of those that a mesh axis runs over, the one named last changes fastest.
Arguments:
- state: float32 [2, 4, 256, 64, 128], P('section', None, 'stream', 'slab'), may hold values from -6 to 6
- source_mask: int32 [16, 4], P(None, 'slab'), may hold values 0 or 1
- deriv_x: float32 [256, 256], replicated, may hold values from -0.28125 to 0.28125
- deriv_z: float32 [128, 128], replicated, may hold values from -0.397747564 to 0.397747564
- filter_x: float32 [256, 256], replicated, may hold values from -0.375 to 0.375
- filter_z: float32 [128, 128], replicated, may hold values from -0.5 to 0.5
Outputs:
- advanced: float32 [2, 4, 256, 64, 128], P('section', None, 'stream', 'slab')
All inputs are finite; a program needn't handle non-finite values. No bound on the sum of `source_mask` on one device may be relied on, other than what follows from the above.
Results may differ from a plain program's by a relative error of at most 0.0001.
Values sent between devices are 32-bit elements; how exact they have to be, the bound alone decides.
A program may use at most 128 MiB of HBM per device.

v0:
```python
import jax
import jax.numpy as jnp
from jax import lax
from jax.sharding import PartitionSpec as P

SEGMENTS = 8
MBLK = 16


mach_number = 0.5
time_step = 0.05
filter_weight = 0.25


def shifted_2(value, axis, steps):
    count = lax.axis_size(axis)
    leading, last = (max(0, -steps), min(count, count - steps))
    return lax.ppermute(value, axis, [(source, source + steps) for source in range(leading, last)])


def with_halo(cells, sides, width):
    for axis, dim in sides:
        count = lax.axis_size(axis)
        ends = count - 1
        head = lax.slice_in_dim(cells, 0, width, axis=dim)
        tail = lax.slice_in_dim(cells, cells.shape[dim] - width, cells.shape[dim], axis=dim)
        cells = jnp.concatenate(
            [
                lax.ppermute(tail, axis, [(i, (i + 1) % count) for i in range(ends)]),
                cells,
                lax.ppermute(head, axis, [((i + 1) % count, i) for i in range(ends)]),
            ],
            axis=dim,
        )
    return cells


def along_x(matrix, fields):
    return jnp.einsum("ij,fjyz->fiyz", matrix, fields, precision=lax.Precision.HIGHEST)


def along_z(matrix, fields):
    return jnp.einsum("fxyz,kz->fxyk", fields, matrix, precision=lax.Precision.HIGHEST)


def padded_slope(padded_one, which_dim):
    upper_cut = [slice(1, -1), slice(1, -1), slice(1, -1)]
    lower_cut = [slice(1, -1), slice(1, -1), slice(1, -1)]
    upper_cut[which_dim] = slice(2, None)
    lower_cut[which_dim] = slice(None, -2)
    return 0.5 * (padded_one[tuple(upper_cut)] - padded_one[tuple(lower_cut)])


def lamb_padded(padded, order):
    dim_x, dim_y, dim_z = order
    speed_x, speed_y, speed_z = (padded[0], padded[1], padded[2])
    center_x = speed_x[1:-1, 1:-1, 1:-1]
    center_y = speed_y[1:-1, 1:-1, 1:-1]
    center_z = speed_z[1:-1, 1:-1, 1:-1]
    vortex_x = padded_slope(speed_z, dim_y) - padded_slope(speed_y, dim_z)
    vortex_y = padded_slope(speed_x, dim_z) - padded_slope(speed_z, dim_x)
    vortex_z = padded_slope(speed_y, dim_x) - padded_slope(speed_x, dim_y)
    return jnp.stack(
        [
            vortex_y * center_z - vortex_z * center_y,
            vortex_z * center_x - vortex_x * center_z,
            vortex_x * center_y - vortex_y * center_x,
        ]
    )


def exchange_source(region_cells, padded, order):
    own_source = -region_cells * lamb_padded(padded, order)
    return shifted_2(own_source, "section", 1)


def slope_in_y(fields):
    padded = with_halo(fields, (("slab", 2),), 2)
    length = fields.shape[2]

    def shifted(offset):
        return lax.slice_in_dim(padded, 2 + offset, 2 + offset + length, axis=2)

    return (8.0 * (shifted(1) - shifted(-1)) - (shifted(2) - shifted(-2))) / 12.0


def tendency(slope_x, slope_y, slope_z, forcing):
    press_rate = -mach_number * slope_x[0] - slope_x[1] - slope_y[1] - slope_z[1]
    axial_rate = -mach_number * slope_x[1] - slope_x[0] + forcing[0]
    normal_rate = -mach_number * slope_x[2] - slope_y[0] + forcing[1]
    third_rate = -mach_number * slope_x[3] - slope_z[0] + forcing[2]
    return jnp.stack([press_rate, axial_rate, normal_rate, third_rate])


def block_x(matrix, fields):
    return lax.all_to_all(
        along_x(matrix, lax.all_to_all(fields, "stream", split_axis=2, concat_axis=1, tiled=True)),
        "stream",
        split_axis=1,
        concat_axis=2,
        tiled=True,
    )


def shards(state, source_mask, deriv_x, deriv_z, filter_x, filter_z):
    fields = state[0]
    blocks = source_mask.astype(jnp.float32)
    block_rows = blocks.shape[0]
    block_cols = blocks.shape[1]
    region = jnp.broadcast_to(blocks[:, None, :, None], (block_rows, MBLK, block_cols, MBLK))
    region = region.reshape(block_rows * MBLK, block_cols * MBLK)
    forcing = None
    width_x = fields.shape[1]
    region = lax.dynamic_slice_in_dim(region, lax.axis_index("stream") * width_x, width_x, 0)
    region_cells = region[None, :, :, None]
    for segment_index in range(SEGMENTS):
        if segment_index % 2 == 0:
            padded = with_halo(fields[1:4], (("stream", 1), ("slab", 2)), 1)
            padded = jnp.pad(padded, ((0, 0), (0, 0), (0, 0), (1, 1)))
            forcing = exchange_source(region_cells, padded, (0, 1, 2))
        slope_x = block_x(deriv_x, fields)
        slope_y = slope_in_y(jnp.stack([fields[0], fields[2]]))
        slope_z = along_z(deriv_z, jnp.stack([fields[0], fields[3]]))
        fields = fields + time_step * tendency(slope_x, slope_y, slope_z, forcing)
    result = (
        fields
        + filter_weight * block_x(filter_x, fields)
        + filter_weight * along_z(filter_z, fields)
    )
    return result[None]


def solution(mesh):
    placed = (P("section", None, "stream", "slab", None), P(None, "slab"), P(), P(), P(), P())
    return jax.shard_map(
        shards,
        mesh=mesh,
        in_specs=placed,
        out_specs=P("section", None, "stream", "slab", None),
        check_vma=False,
    )
```

profile of v0, /device:TPU:16, one launch (start us, length us, event | category | flops | bytes accessed | tf_op | source)
XLA Modules:
  0.0 721.5 jit_solution(7689165804297841041)
XLA Ops:
  9.5 5.0 all-to-all-start
  26.4 4.3 select_maximum_fusion.12
  34.1 6.5 all-to-all-done
  42.3 5.0 convolution_bitcast_fusion.8
  50.4 4.4 all-to-all-start.1
  72.9 7.3 %all-to-all-done.1 = f32[4,256,4,128]{3,2,0,1:T(4,128)} async-done(((f32[4,256,4,128]{3,2,0,1:T(4,128)}), f32[4,256,4,128]{3,2,0,1:T(4,128)}, u32[]{:S(2)}, u32[]{:S(2)}) %all-to-all-start.1) | async-done | bytes 2097184 | tf_op jit(solution)/shard_map/all_to_all | solution.py:96
  88.3 27.4 %all_to_all.291 = f32[4,64,16,128]{3,1,0,2:T(8,128)S(1)} all-to-all(f32[4,64,16,128]{3,1,0,2:T(8,128)S(1)} %copy.188), channel_id=1, replica_groups=mesh['section'=2,'stream'=4,'slab'=4] {'stream'}, dimensions={2} | all-to-all | bytes 4194304 | tf_op jit(solution)/shard_map/all_to_all | solution.py:97
  115.9 5.0 convolution_bitcast_fusion.7
  124.0 4.4 all-to-all-start.3
  132.5 3.9 collective-permute-start.8
  140.9 10.6 %all-to-all-done.3 = f32[4,256,4,128]{3,2,0,1:T(4,128)} async-done(((f32[4,256,4,128]{3,2,0,1:T(4,128)}), f32[4,256,4,128]{3,2,0,1:T(4,128)}, u32[]{:S(2)}, u32[]{:S(2)}) %all-to-all-start.3) | async-done | bytes 2097184 | tf_op jit(solution)/shard_map/all_to_all | solution.py:96
  163.6 4.2 collective-permute-done.12
  176.5 4.6 all-to-all-start.4
  181.1 5.6 select_maximum_fusion.8
  191.1 11.8 %all-to-all-done.4 = f32[4,64,16,128]{3,1,0,2:T(8,128)} async-done(((f32[4,64,16,128]{3,1,0,2:T(8,128)}), f32[4,64,16,128]{3,1,0,2:T(8,128)}, u32[]{:S(2)}, u32[]{:S(2)}) %all-to-all-start.4) | async-done | bytes 2097184 | tf_op jit(solution)/shard_map/all_to_all | solution.py:97
  204.6 5.0 convolution_bitcast_fusion.6
  212.6 4.5 all-to-all-start.5
  235.2 5.4 all-to-all-done.5
  249.3 27.3 %all_to_all.292 = f32[4,64,16,128]{3,1,0,2:T(8,128)S(1)} all-to-all(f32[4,64,16,128]{3,1,0,2:T(8,128)S(1)} %copy.208), channel_id=1, replica_groups=mesh['section'=2,'stream'=4,'slab'=4] {'stream'}, dimensions={2} | all-to-all | bytes 4194304 | tf_op jit(solution)/shard_map/all_to_all | solution.py:97
  276.8 5.0 convolution_bitcast_fusion.5
  284.9 4.4 all-to-all-start.7
  302.4 9.9 %all-to-all-done.7 = f32[4,256,4,128]{3,2,0,1:T(4,128)} async-done(((f32[4,256,4,128]{3,2,0,1:T(4,128)}), f32[4,256,4,128]{3,2,0,1:T(4,128)}, u32[]{:S(2)}, u32[]{:S(2)}) %all-to-all-start.7) | async-done | bytes 2097184 | tf_op jit(solution)/shard_map/all_to_all | solution.py:96
  325.2 4.2 collective-permute-done.21
  330.2 4.1 collective-permute-start.22
  338.2 4.6 all-to-all-start.8
  342.9 5.6 select_maximum_fusion.4
  352.9 12.0 %all-to-all-done.8 = f32[4,64,16,128]{3,1,0,2:T(8,128)} async-done(((f32[4,64,16,128]{3,1,0,2:T(8,128)}), f32[4,64,16,128]{3,1,0,2:T(8,128)}, u32[]{:S(2)}, u32[]{:S(2)}) %all-to-all-start.8) | async-done | bytes 2097184 | tf_op jit(solution)/shard_map/all_to_all | solution.py:97
  366.6 5.0 convolution_bitcast_fusion.4
  374.6 4.5 all-to-all-start.9
  397.4 5.3 all-to-all-done.9
  413.4 27.3 %all_to_all.293 = f32[4,64,16,128]{3,1,0,2:T(8,128)S(1)} all-to-all(f32[4,64,16,128]{3,1,0,2:T(8,128)S(1)} %copy.228), channel_id=1, replica_groups=mesh['section'=2,'stream'=4,'slab'=4] {'stream'}, dimensions={2} | all-to-all | bytes 4194304 | tf_op jit(solution)/shard_map/all_to_all | solution.py:97
  441.0 5.0 convolution_bitcast_fusion.3
  449.1 4.4 all-to-all-start.11
  466.8 9.7 %all-to-all-done.11 = f32[4,256,4,128]{3,2,0,1:T(4,128)} async-done(((f32[4,256,4,128]{3,2,0,1:T(4,128)}), f32[4,256,4,128]{3,2,0,1:T(4,128)}, u32[]{:S(2)}, u32[]{:S(2)}) %all-to-all-start.11) | async-done | bytes 2097184 | tf_op jit(solution)/shard_map/all_to_all | solution.py:96
  491.1 4.2 collective-permute-done.30
  496.1 4.3 collective-permute-start.31
  504.3 4.6 all-to-all-start.12
  509.0 5.6 select_maximum_fusion
  518.9 12.0 %all-to-all-done.12 = f32[4,64,16,128]{3,1,0,2:T(8,128)} async-done(((f32[4,64,16,128]{3,1,0,2:T(8,128)}), f32[4,64,16,128]{3,1,0,2:T(8,128)}, u32[]{:S(2)}, u32[]{:S(2)}) %all-to-all-start.12) | async-done | bytes 2097184 | tf_op jit(solution)/shard_map/all_to_all | solution.py:97
  532.7 5.0 convolution_bitcast_fusion.2
  540.7 4.5 all-to-all-start.13
  563.5 5.3 all-to-all-done.13
  580.0 27.3 %all_to_all.294 = f32[4,64,16,128]{3,1,0,2:T(8,128)S(1)} all-to-all(f32[4,64,16,128]{3,1,0,2:T(8,128)S(1)} %copy.248), channel_id=1, replica_groups=mesh['section'=2,'stream'=4,'slab'=4] {'stream'}, dimensions={2} | all-to-all | bytes 4194304 | tf_op jit(solution)/shard_map/all_to_all | solution.py:97
  607.6 5.0 convolution_bitcast_fusion.1
  615.7 4.4 all-to-all-start.15
  633.4 9.7 %all-to-all-done.15 = f32[4,256,4,128]{3,2,0,1:T(4,128)} async-done(((f32[4,256,4,128]{3,2,0,1:T(4,128)}), f32[4,256,4,128]{3,2,0,1:T(4,128)}, u32[]{:S(2)}, u32[]{:S(2)}) %all-to-all-start.15) | async-done | bytes 2097184 | tf_op jit(solution)/shard_map/all_to_all | solution.py:96
  654.2 27.3 %all_to_all.295 = f32[4,64,16,128]{3,1,0,2:T(8,128)S(1)} all-to-all(f32[4,64,16,128]{3,1,0,2:T(8,128)S(1)} %copy.258), channel_id=1, replica_groups=mesh['section'=2,'stream'=4,'slab'=4] {'stream'}, dimensions={2} | all-to-all | bytes 4194304 | tf_op jit(solution)/shard_map/all_to_all | solution.py:97
  688.2 27.3 %all_to_all.296 = f32[4,256,4,128]{3,2,0,1:T(4,128)S(1)} all-to-all(f32[4,256,4,128]{3,2,0,1:T(4,128)} %copy.262), channel_id=1, replica_groups=mesh['section'=2,'stream'=4,'slab'=4] {'stream'}, dimensions={1} | all-to-all | bytes 4194304 | tf_op jit(solution)/shard_map/all_to_all | solution.py:96
  (593 shorter events, 308.1 us)
Async XLA Ops:
  2.8 11.8 %collective-permute-start.2 = (f32[3,1,16,128]{3,2,1,0:T(8,128)S(1)}, f32[3,1,16,128]{3,2,1,0:T(8,128)S(1)}, u32[]{:S(2)}, u32[]{:S(2)}) collective-permute-start(f32[3,1,16,128]{3,2,1,0:T(8,128)S(1)} %get-tuple-element.139), channel_id=1, source_target_pairs={{0,4},{4,8},{8,12},{1,5},{5,9},{9,13},{2,6},{6,10},{10,14},{3,7},{... | collective-permute-start | bytes 73736 | tf_op jit(solution)/shard_map/ppermute | solution.py:29
  6.2 8.4 %collective-permute-start.3 = (f32[3,1,16,128]{3,2,1,0:T(8,128)S(1)}, f32[3,1,16,128]{3,2,1,0:T(8,128)S(1)}, u32[]{:S(2)}, u32[]{:S(2)}) collective-permute-start(f32[3,1,16,128]{3,2,1,0:T(8,128)S(1)} %get-tuple-element.140), channel_id=1, source_target_pairs={{4,0},{8,4},{12,8},{5,1},{9,5},{13,9},{6,2},{10,6},{14,10},{7,3},{... | collective-permute-start | bytes 73736 | tf_op jit(solution)/shard_map/ppermute | solution.py:31
  9.5 31.0 %all-to-all-start = ((f32[4,64,16,128]{3,1,0,2:T(8,128)}), f32[4,64,16,128]{3,1,0,2:T(8,128)}, u32[]{:S(2)}, u32[]{:S(2)}) async-start(f32[4,64,16,128]{3,1,0,2:T(8,128)} %copy.178), calls=%async_computation | async-start | bytes 4194304 | tf_op jit(solution)/shard_map/all_to_all | solution.py:97
  16.4 6.5 collective-permute-start.4
  19.9 6.5 collective-permute-start.5
  50.4 29.8 %all-to-all-start.1 = ((f32[4,256,4,128]{3,2,0,1:T(4,128)}), f32[4,256,4,128]{3,2,0,1:T(4,128)}, u32[]{:S(2)}, u32[]{:S(2)}) async-start(f32[4,256,4,128]{3,2,0,1:T(4,128)} %copy.182), calls=%async_computation.1 | async-start | bytes 4194304 | tf_op jit(solution)/shard_map/all_to_all | solution.py:96
  58.7 25.4 %collective-permute-start.6 = (f32[3,64,16,128]{3,2,1,0:T(8,128)}, f32[3,64,16,128]{3,2,1,0:T(8,128)}, u32[]{:S(2)}, u32[]{:S(2)}) collective-permute-start(f32[3,64,16,128]{3,2,1,0:T(8,128)} %maximum_multiply_fusion.8), channel_id=1, source_target_pairs={{0,16},{1,17},{2,18},{3,19},{4,20},{5,21},{6,22},{7,23},{8,24},{9,... | collective-permute-start | bytes 4718600 | tf_op jit(solution)/shard_map/ppermute | solution.py:18
  62.0 8.1 %collective-permute-start = (f32[2,64,2,128]{3,2,1,0:T(2,128)S(1)}, f32[2,64,2,128]{3,2,1,0:T(2,128)S(1)}, u32[]{:S(2)}, u32[]{:S(2)}) collective-permute-start(f32[2,64,2,128]{3,2,1,0:T(2,128)S(1)} %get-tuple-element.171), channel_id=1, source_target_pairs={{1,0},{2,1},{3,2},{5,4},{6,5},{7,6},{9,8},{10,9},{11,10},{13,12},{... | collective-permute-start | bytes 393224 | tf_op jit(solution)/shard_map/ppermute | solution.py:31
  64.4 6.9 collective-permute-start.1
  124.0 27.5 %all-to-all-start.3 = ((f32[4,256,4,128]{3,2,0,1:T(4,128)}), f32[4,256,4,128]{3,2,0,1:T(4,128)}, u32[]{:S(2)}, u32[]{:S(2)}) async-start(f32[4,256,4,128]{3,2,0,1:T(4,128)} %copy.192), calls=%async_computation.3 | async-start | bytes 4194304 | tf_op jit(solution)/shard_map/all_to_all | solution.py:96
  130.1 8.2 %collective-permute-start.7 = (f32[2,64,2,128]{3,2,1,0:T(2,128)S(1)}, f32[2,64,2,128]{3,2,1,0:T(2,128)S(1)}, u32[]{:S(2)}, u32[]{:S(2)}) collective-permute-start(f32[2,64,2,128]{3,2,1,0:T(2,128)S(1)} %get-tuple-element.167), channel_id=1, source_target_pairs={{1,0},{2,1},{3,2},{5,4},{6,5},{7,6},{9,8},{10,9},{11,10},{13,12},{... | collective-permute-start | bytes 393224 | tf_op jit(solution)/shard_map/ppermute | solution.py:31
  132.5 6.9 collective-permute-start.8
  158.8 4.8 collective-permute-start.11
  162.1 5.7 collective-permute-start.12
  168.7 12.5 %collective-permute-start.13 = (f32[3,66,1,128]{3,2,1,0:T(1,128)}, f32[3,66,1,128]{3,2,1,0:T(1,128)}, u32[]{:S(2)}, u32[]{:S(2)}) collective-permute-start(f32[3,66,1,128]{3,2,1,0:T(1,128)} %get-tuple-element.103), channel_id=1, source_target_pairs={{0,1},{1,2},{2,3},{4,5},{5,6},{6,7},{8,9},{9,10},{10,11},{12,13},{... | collective-permute-start | bytes 304136 | tf_op jit(solution)/shard_map/ppermute | solution.py:29
  172.1 9.0 %collective-permute-start.14 = (f32[3,66,1,128]{3,2,1,0:T(1,128)}, f32[3,66,1,128]{3,2,1,0:T(1,128)}, u32[]{:S(2)}, u32[]{:S(2)}) collective-permute-start(f32[3,66,1,128]{3,2,1,0:T(1,128)} %get-tuple-element.104), channel_id=1, source_target_pairs={{1,0},{2,1},{3,2},{5,4},{6,5},{7,6},{9,8},{10,9},{11,10},{13,12},{... | collective-permute-start | bytes 304136 | tf_op jit(solution)/shard_map/ppermute | solution.py:31
  176.5 26.4 %all-to-all-start.4 = ((f32[4,64,16,128]{3,1,0,2:T(8,128)}), f32[4,64,16,128]{3,1,0,2:T(8,128)}, u32[]{:S(2)}, u32[]{:S(2)}) async-start(f32[4,64,16,128]{3,1,0,2:T(8,128)} %copy.198), calls=%async_computation.4 | async-start | bytes 4194304 | tf_op jit(solution)/shard_map/all_to_all | solution.py:97
  212.6 28.1 %all-to-all-start.5 = ((f32[4,256,4,128]{3,2,0,1:T(4,128)}), f32[4,256,4,128]{3,2,0,1:T(4,128)}, u32[]{:S(2)}, u32[]{:S(2)}) async-start(f32[4,256,4,128]{3,2,0,1:T(4,128)} %copy.202), calls=%async_computation.5 | async-start | bytes 4194304 | tf_op jit(solution)/shard_map/all_to_all | solution.py:96
  221.0 23.6 %collective-permute-start.15 = (f32[3,64,16,128]{3,2,1,0:T(8,128)}, f32[3,64,16,128]{3,2,1,0:T(8,128)}, u32[]{:S(2)}, u32[]{:S(2)}) collective-permute-start(f32[3,64,16,128]{3,2,1,0:T(8,128)} %maximum_multiply_fusion.9), channel_id=1, source_target_pairs={{0,16},{1,17},{2,18},{3,19},{4,20},{5,21},{6,22},{7,23},{8,24},{9,... | collective-permute-start | bytes 4718600 | tf_op jit(solution)/shard_map/ppermute | solution.py:18
  223.7 8.1 %collective-permute-start.9 = (f32[2,64,2,128]{3,2,1,0:T(2,128)S(1)}, f32[2,64,2,128]{3,2,1,0:T(2,128)S(1)}, u32[]{:S(2)}, u32[]{:S(2)}) collective-permute-start(f32[2,64,2,128]{3,2,1,0:T(2,128)S(1)} %get-tuple-element.163), channel_id=1, source_target_pairs={{1,0},{2,1},{3,2},{5,4},{6,5},{7,6},{9,8},{10,9},{11,10},{13,12},{... | collective-permute-start | bytes 393224 | tf_op jit(solution)/shard_map/ppermute | solution.py:31
  226.7 6.9 collective-permute-start.10
  284.9 27.4 %all-to-all-start.7 = ((f32[4,256,4,128]{3,2,0,1:T(4,128)}), f32[4,256,4,128]{3,2,0,1:T(4,128)}, u32[]{:S(2)}, u32[]{:S(2)}) async-start(f32[4,256,4,128]{3,2,0,1:T(4,128)} %copy.212), calls=%async_computation.7 | async-start | bytes 4194304 | tf_op jit(solution)/shard_map/all_to_all | solution.py:96
  291.0 8.2 %collective-permute-start.16 = (f32[2,64,2,128]{3,2,1,0:T(2,128)S(1)}, f32[2,64,2,128]{3,2,1,0:T(2,128)S(1)}, u32[]{:S(2)}, u32[]{:S(2)}) collective-permute-start(f32[2,64,2,128]{3,2,1,0:T(2,128)S(1)} %get-tuple-element.159), channel_id=1, source_target_pairs={{1,0},{2,1},{3,2},{5,4},{6,5},{7,6},{9,8},{10,9},{11,10},{13,12},{... | collective-permute-start | bytes 393224 | tf_op jit(solution)/shard_map/ppermute | solution.py:31
  294.0 6.9 collective-permute-start.17
  320.4 4.8 collective-permute-start.20
  323.7 5.7 collective-permute-start.21
  330.2 12.6 %collective-permute-start.22 = (f32[3,66,1,128]{3,2,1,0:T(1,128)}, f32[3,66,1,128]{3,2,1,0:T(1,128)}, u32[]{:S(2)}, u32[]{:S(2)}) collective-permute-start(f32[3,66,1,128]{3,2,1,0:T(1,128)} %get-tuple-element.101), channel_id=1, source_target_pairs={{0,1},{1,2},{2,3},{4,5},{5,6},{6,7},{8,9},{9,10},{10,11},{12,13},{... | collective-permute-start | bytes 304136 | tf_op jit(solution)/shard_map/ppermute | solution.py:29
  334.3 8.5 %collective-permute-start.23 = (f32[3,66,1,128]{3,2,1,0:T(1,128)}, f32[3,66,1,128]{3,2,1,0:T(1,128)}, u32[]{:S(2)}, u32[]{:S(2)}) collective-permute-start(f32[3,66,1,128]{3,2,1,0:T(1,128)} %get-tuple-element.102), channel_id=1, source_target_pairs={{1,0},{2,1},{3,2},{5,4},{6,5},{7,6},{9,8},{10,9},{11,10},{13,12},{... | collective-permute-start | bytes 304136 | tf_op jit(solution)/shard_map/ppermute | solution.py:31
  338.2 26.6 %all-to-all-start.8 = ((f32[4,64,16,128]{3,1,0,2:T(8,128)}), f32[4,64,16,128]{3,1,0,2:T(8,128)}, u32[]{:S(2)}, u32[]{:S(2)}) async-start(f32[4,64,16,128]{3,1,0,2:T(8,128)} %copy.218), calls=%async_computation.8 | async-start | bytes 4194304 | tf_op jit(solution)/shard_map/all_to_all | solution.py:97
  374.6 28.1 %all-to-all-start.9 = ((f32[4,256,4,128]{3,2,0,1:T(4,128)}), f32[4,256,4,128]{3,2,0,1:T(4,128)}, u32[]{:S(2)}, u32[]{:S(2)}) async-start(f32[4,256,4,128]{3,2,0,1:T(4,128)} %copy.222), calls=%async_computation.9 | async-start | bytes 4194304 | tf_op jit(solution)/shard_map/all_to_all | solution.py:96
  383.1 23.6 %collective-permute-start.24 = (f32[3,64,16,128]{3,2,1,0:T(8,128)}, f32[3,64,16,128]{3,2,1,0:T(8,128)}, u32[]{:S(2)}, u32[]{:S(2)}) collective-permute-start(f32[3,64,16,128]{3,2,1,0:T(8,128)} %maximum_multiply_fusion.10), channel_id=1, source_target_pairs={{0,16},{1,17},{2,18},{3,19},{4,20},{5,21},{6,22},{7,23},{8,24},{9,... | collective-permute-start | bytes 4718600 | tf_op jit(solution)/shard_map/ppermute | solution.py:18
  385.7 8.1 %collective-permute-start.18 = (f32[2,64,2,128]{3,2,1,0:T(2,128)S(1)}, f32[2,64,2,128]{3,2,1,0:T(2,128)S(1)}, u32[]{:S(2)}, u32[]{:S(2)}) collective-permute-start(f32[2,64,2,128]{3,2,1,0:T(2,128)S(1)} %get-tuple-element.155), channel_id=1, source_target_pairs={{1,0},{2,1},{3,2},{5,4},{6,5},{7,6},{9,8},{10,9},{11,10},{13,12},{... | collective-permute-start | bytes 393224 | tf_op jit(solution)/shard_map/ppermute | solution.py:31
  388.9 6.9 collective-permute-start.19
  449.1 27.4 %all-to-all-start.11 = ((f32[4,256,4,128]{3,2,0,1:T(4,128)}), f32[4,256,4,128]{3,2,0,1:T(4,128)}, u32[]{:S(2)}, u32[]{:S(2)}) async-start(f32[4,256,4,128]{3,2,0,1:T(4,128)} %copy.232), calls=%async_computation.11 | async-start | bytes 4194304 | tf_op jit(solution)/shard_map/all_to_all | solution.py:96
  455.1 8.2 %collective-permute-start.25 = (f32[2,64,2,128]{3,2,1,0:T(2,128)S(1)}, f32[2,64,2,128]{3,2,1,0:T(2,128)S(1)}, u32[]{:S(2)}, u32[]{:S(2)}) collective-permute-start(f32[2,64,2,128]{3,2,1,0:T(2,128)S(1)} %get-tuple-element.151), channel_id=1, source_target_pairs={{1,0},{2,1},{3,2},{5,4},{6,5},{7,6},{9,8},{10,9},{11,10},{13,12},{... | collective-permute-start | bytes 393224 | tf_op jit(solution)/shard_map/ppermute | solution.py:31
  458.3 6.9 collective-permute-start.26
  486.3 4.8 collective-permute-start.29
  489.6 5.7 collective-permute-start.30
  496.1 12.8 %collective-permute-start.31 = (f32[3,66,1,128]{3,2,1,0:T(1,128)}, f32[3,66,1,128]{3,2,1,0:T(1,128)}, u32[]{:S(2)}, u32[]{:S(2)}) collective-permute-start(f32[3,66,1,128]{3,2,1,0:T(1,128)} %get-tuple-element.99), channel_id=1, source_target_pairs={{0,1},{1,2},{2,3},{4,5},{5,6},{6,7},{8,9},{9,10},{10,11},{12,13},{... | collective-permute-start | bytes 304136 | tf_op jit(solution)/shard_map/ppermute | solution.py:29
  500.4 8.5 %collective-permute-start.32 = (f32[3,66,1,128]{3,2,1,0:T(1,128)}, f32[3,66,1,128]{3,2,1,0:T(1,128)}, u32[]{:S(2)}, u32[]{:S(2)}) collective-permute-start(f32[3,66,1,128]{3,2,1,0:T(1,128)} %get-tuple-element.100), channel_id=1, source_target_pairs={{1,0},{2,1},{3,2},{5,4},{6,5},{7,6},{9,8},{10,9},{11,10},{13,12},{... | collective-permute-start | bytes 304136 | tf_op jit(solution)/shard_map/ppermute | solution.py:31
  504.3 26.6 %all-to-all-start.12 = ((f32[4,64,16,128]{3,1,0,2:T(8,128)}), f32[4,64,16,128]{3,1,0,2:T(8,128)}, u32[]{:S(2)}, u32[]{:S(2)}) async-start(f32[4,64,16,128]{3,1,0,2:T(8,128)} %copy.238), calls=%async_computation.12 | async-start | bytes 4194304 | tf_op jit(solution)/shard_map/all_to_all | solution.py:97
  540.7 28.1 %all-to-all-start.13 = ((f32[4,256,4,128]{3,2,0,1:T(4,128)}), f32[4,256,4,128]{3,2,0,1:T(4,128)}, u32[]{:S(2)}, u32[]{:S(2)}) async-start(f32[4,256,4,128]{3,2,0,1:T(4,128)} %copy.242), calls=%async_computation.13 | async-start | bytes 4194304 | tf_op jit(solution)/shard_map/all_to_all | solution.py:96
  549.1 23.5 %collective-permute-start.33 = (f32[3,64,16,128]{3,2,1,0:T(8,128)}, f32[3,64,16,128]{3,2,1,0:T(8,128)}, u32[]{:S(2)}, u32[]{:S(2)}) collective-permute-start(f32[3,64,16,128]{3,2,1,0:T(8,128)} %maximum_multiply_fusion.11), channel_id=1, source_target_pairs={{0,16},{1,17},{2,18},{3,19},{4,20},{5,21},{6,22},{7,23},{8,24},{9,... | collective-permute-start | bytes 4718600 | tf_op jit(solution)/shard_map/ppermute | solution.py:18
  551.8 8.1 %collective-permute-start.27 = (f32[2,64,2,128]{3,2,1,0:T(2,128)S(1)}, f32[2,64,2,128]{3,2,1,0:T(2,128)S(1)}, u32[]{:S(2)}, u32[]{:S(2)}) collective-permute-start(f32[2,64,2,128]{3,2,1,0:T(2,128)S(1)} %get-tuple-element.147), channel_id=1, source_target_pairs={{1,0},{2,1},{3,2},{5,4},{6,5},{7,6},{9,8},{10,9},{11,10},{13,12},{... | collective-permute-start | bytes 393224 | tf_op jit(solution)/shard_map/ppermute | solution.py:31
  555.0 6.9 collective-permute-start.28
  615.7 27.4 %all-to-all-start.15 = ((f32[4,256,4,128]{3,2,0,1:T(4,128)}), f32[4,256,4,128]{3,2,0,1:T(4,128)}, u32[]{:S(2)}, u32[]{:S(2)}) async-start(f32[4,256,4,128]{3,2,0,1:T(4,128)} %copy.252), calls=%async_computation.15 | async-start | bytes 4194304 | tf_op jit(solution)/shard_map/all_to_all | solution.py:96
  621.7 8.1 %collective-permute-start.34 = (f32[2,64,2,128]{3,2,1,0:T(2,128)S(1)}, f32[2,64,2,128]{3,2,1,0:T(2,128)S(1)}, u32[]{:S(2)}, u32[]{:S(2)}) collective-permute-start(f32[2,64,2,128]{3,2,1,0:T(2,128)S(1)} %get-tuple-element.143), channel_id=1, source_target_pairs={{1,0},{2,1},{3,2},{5,4},{6,5},{7,6},{9,8},{10,9},{11,10},{13,12},{... | collective-permute-start | bytes 393224 | tf_op jit(solution)/shard_map/ppermute | solution.py:31
  624.9 6.9 collective-permute-start.35
  (178 other events, 568.2 us)
where the time goes:
time: 734 us; the launch traced here: 721 us
  blocking collectives  164 us (22%)
  starting transfers between devices  156 us (21%)
  waiting for transfers between devices  136 us (19%)
  local copies, waits for them, and re-layouts  105 us (14%)
  other arithmetic  94.3 us (13%)
  matrix products  62.3 us (8%)
    all_to_all x5, blocking collectives, block_x(): lax.all_to_all(fields, 'stream', split_axis=2, concat_axis=1, tiled=True)  137 us
    all_to_all x8, waiting for transfers between devices, block_x(): lax.all_to_all(along_x(matrix, lax.all_to_all(fields, 'stream', split_axi...  63.2 us
    ppermute x16, starting transfers between devices, with_halo(): lax.ppermute(tail, axis, [(i, (i + 1) % count) for i in range(ends)])  54.5 us
    dot_general x9, matrix products, along_x(): jnp.einsum('ij,fjyz->fiyz', matrix, fields, precision=lax.Precision.HIGHEST)  43.2 us
    all_to_all x4, waiting for transfers between devices, block_x(): lax.all_to_all(fields, 'stream', split_axis=2, concat_axis=1, tiled=True)  42.3 us
    ppermute x16, starting transfers between devices, with_halo(): lax.ppermute(head, axis, [((i + 1) % count, i) for i in range(ends)])  37 us
    all_to_all x8, starting transfers between devices, block_x(): lax.all_to_all(along_x(matrix, lax.all_to_all(fields, 'stream', split_axi...  35.6 us
    all_to_all x1, blocking collectives, block_x(): lax.all_to_all(along_x(matrix, lax.all_to_all(fields, 'stream', split_axi...  27.3 us
  transfers between devices with their start and end apart: 48, of which 28 were waited for; matrix products, arithmetic and copies ran while one was open for 16% of the time, Pallas kernels for 0%

commit v1 on v0

v1 whole, which is shorter than its diff:
```python
import functools
import math

import jax
import jax.numpy as jnp
from jax import lax
from jax.experimental import pallas as pl
from jax.experimental.pallas import tpu as pltpu
from jax.sharding import PartitionSpec as P

SEGMENTS = 8
MBLK = 16

mach_number = 0.5
time_step = 0.05
filter_weight = 0.25


def split_parts(value):
    high = value.astype(jnp.bfloat16)
    low = (value - high.astype(jnp.float32)).astype(jnp.bfloat16)
    return high, low


def dot_parts(left, right):
    dot = functools.partial(jnp.dot, preferred_element_type=jnp.float32)
    return dot(left[0], right[0]) + (dot(left[0], right[1]) + dot(left[1], right[0]))


def wide(ref):
    return jnp.concatenate([ref[0, i] for i in range(4)], axis=1)


def local_kernel(fields_ref, dx_ref, dzt_ref, out_ref):
    nz = fields_ref.shape[3]
    nx = fields_ref.shape[2]
    dx = split_parts(dx_ref[...])
    dzt = split_parts(dzt_ref[...])
    fields = wide(fields_ref)
    sx = dot_parts(dx, split_parts(fields))
    sz = dot_parts(split_parts(jnp.concatenate([fields_ref[0, 0], fields_ref[0, 3]], axis=0)), dzt)
    sp, su, sv, sw = (sx[:, i * nz:(i + 1) * nz] for i in range(4))
    out_ref[0, 0] = fields_ref[0, 0] - time_step * (mach_number * sp + su + sz[nx:])
    out_ref[0, 1] = fields_ref[0, 1] - time_step * (mach_number * su + sp)
    out_ref[0, 2] = fields_ref[0, 2] - (time_step * mach_number) * sv
    out_ref[0, 3] = fields_ref[0, 3] - time_step * (mach_number * sw + sz[:nx])


def filter_kernel(fields_ref, fx_ref, fzt_ref, out_ref):
    nz = fields_ref.shape[3]
    nx = fields_ref.shape[2]
    fx = split_parts(fx_ref[...])
    fzt = split_parts(fzt_ref[...])
    sx = dot_parts(fx, split_parts(wide(fields_ref)))
    sz = dot_parts(split_parts(jnp.concatenate([fields_ref[0, i] for i in range(4)], axis=0)), fzt)
    for i in range(4):
        out_ref[0, i] = fields_ref[0, i] + filter_weight * (sx[:, i * nz:(i + 1) * nz] + sz[i * nx:(i + 1) * nx])


def row_call(kernel, fields, mat_x, mat_zt):
    rows, count, nx, nz = fields.shape
    block = pl.BlockSpec((1, count, nx, nz), lambda i: (i, 0, 0, 0))
    return pl.pallas_call(
        kernel,
        grid=(rows,),
        in_specs=[block, pl.BlockSpec((nx, nx), lambda i: (0, 0)), pl.BlockSpec((nz, nz), lambda i: (0, 0))],
        out_specs=block,
        out_shape=jax.ShapeDtypeStruct(fields.shape, jnp.float32),
        cost_estimate=pl.CostEstimate(
            flops=6 * rows * count * nx * nz * (nx + nz), bytes_accessed=8 * fields.size, transcendentals=0
        ),
    )(fields, mat_x, mat_zt)


def chain(streams, slabs):
    side = math.isqrt(streams)
    path = list(range(streams))
    if side * side == streams:
        path = [r * side + (c if r % 2 == 0 else side - 1 - c) for r in range(side) for c in range(side)]
    place = [path.index(s) for s in range(streams)]
    order = []
    for k in range(slabs):
        order += [s * slabs + k for s in (path if k % 2 == 0 else path[::-1])]
    return place, order


def neighbour_rows(values, width, order, sections):
    rows = values.shape[0]
    total = len(order)
    axes = ("section", "stream", "slab")

    def shift(part, steps):
        pairs = []
        for section in range(sections):
            for g in range(total):
                if 0 <= g + steps < total:
                    pairs.append((section * total + order[g], section * total + order[g + steps]))
        return lax.ppermute(part, axes, pairs)

    if rows >= width:
        return shift(values[rows - width:], 1), shift(values[:width], -1)
    reach = -(-width // rows)
    before = jnp.concatenate([shift(values, d) for d in range(reach, 0, -1)], axis=0)
    after = jnp.concatenate([shift(values, -d) for d in range(1, reach + 1)], axis=0)
    return before[reach * rows - width:], after[:width]


def slope(values, dim):
    pads = [(0, 0)] * values.ndim
    pads[dim] = (1, 1)
    padded = jnp.pad(values, pads)
    length = values.shape[dim]
    return 0.5 * (
        lax.slice_in_dim(padded, 2, length + 2, axis=dim) - lax.slice_in_dim(padded, 0, length, axis=dim)
    )


def lamb(fields, before, after):
    u, v, w = fields[:, 1], fields[:, 2], fields[:, 3]
    rows = fields.shape[0]
    near = jnp.concatenate([before, jnp.stack([u, w], axis=1), after], axis=0)
    c2 = 0.5 * (near[2:] - near[:rows])
    ox = c2[:, 1] - slope(v, 2)
    oy = slope(u, 2) - slope(w, 1)
    oz = slope(v, 1) - c2[:, 0]
    return jnp.stack([oy * w - oz * v, oz * u - ox * w, ox * v - oy * u], axis=1)


def shards(state, source_mask, deriv_x, deriv_z, filter_x, filter_z):
    streams, slabs = lax.axis_size("stream"), lax.axis_size("slab")
    place, order = chain(streams, slabs)
    fields = state[0]
    count, width_x, width_y, nz = fields.shape
    nx = width_x * streams
    rows = width_y // streams
    even = lax.axis_index("slab") % 2 == 0
    back = [streams - 1 - p for p in place]

    parts = fields.reshape(count, width_x, streams, rows, nz).transpose(2, 3, 0, 1, 4)
    parts = jnp.where(even, jnp.stack([parts[p] for p in place]), jnp.stack([parts[p] for p in back]))
    parts = lax.all_to_all(parts, "stream", split_axis=0, concat_axis=0, tiled=True)
    fields = parts.transpose(1, 2, 0, 3, 4).reshape(rows, count, nx, nz)

    blocks = source_mask.astype(jnp.float32)
    region = jnp.repeat(jnp.repeat(blocks, MBLK, axis=0), MBLK, axis=1).T
    mine = jnp.asarray(place)[lax.axis_index("stream")]
    mine = jnp.where(even, mine, streams - 1 - mine)
    region = lax.dynamic_slice_in_dim(region, mine * rows, rows, 0)[:, None, :, None]
    deriv_zt, filter_zt = deriv_z.T, filter_z.T

    forcing = None
    for segment in range(SEGMENTS):
        pv = jnp.stack([fields[:, 0], fields[:, 2]], axis=1)
        before, after = neighbour_rows(pv, 2, order, 2)
        if segment % 2 == 0:
            uw = jnp.stack([fields[:, 1], fields[:, 3]], axis=1)
            low, high = neighbour_rows(uw, 1, order, 1)
            source = -region * lamb(fields, low, high)
            forcing = lax.ppermute(source, "section", [(0, 1)])
        part = row_call(local_kernel, fields, deriv_x, deriv_zt)
        near = jnp.concatenate([before, pv, after], axis=0)
        dy = (8.0 * (near[3:3 + rows] - near[1:1 + rows]) - (near[4:4 + rows] - near[:rows])) / 12.0
        fields = jnp.stack(
            [
                part[:, 0] - time_step * dy[:, 1],
                part[:, 1] + time_step * forcing[:, 0],
                part[:, 2] + time_step * (forcing[:, 1] - dy[:, 0]),
                part[:, 3] + time_step * forcing[:, 2],
            ],
            axis=1,
        )
    fields = row_call(filter_kernel, fields, filter_x, filter_zt)

    parts = fields.reshape(rows, count, streams, width_x, nz).transpose(2, 0, 1, 3, 4)
    parts = lax.all_to_all(parts, "stream", split_axis=0, concat_axis=0, tiled=True)
    inv_place = [place.index(j) for j in range(streams)]
    inv_back = [back.index(j) for j in range(streams)]
    parts = jnp.where(even, jnp.stack([parts[p] for p in inv_place]), jnp.stack([parts[p] for p in inv_back]))
    return parts.transpose(2, 3, 0, 1, 4).reshape(1, count, width_x, width_y, nz)


def solution(mesh):
    placed = (P("section", None, "stream", "slab", None), P(None, "slab"), P(), P(), P(), P())
    return jax.shard_map(
        shards,
        mesh=mesh,
        in_specs=placed,
        out_specs=P("section", None, "stream", "slab", None),
        check_vma=False,
    )
```

time: 734 us -> 293 us (0.40); the launches traced: 721 us -> 291 us
  blocking collectives: 164 us -> 49 us
  waiting for transfers between devices: 136 us -> 42.3 us
  starting transfers between devices: 156 us -> 78.3 us
  local copies, waits for them, and re-layouts: 105 us -> 35.4 us
  matrix products: 62.3 us -> 0 us
  other arithmetic: 94.3 us -> 42.3 us
  Pallas kernels: 0 us -> 43.1 us
    all_to_all x6 -> x2, blocking collectives: 164 us -> 49 us  [shards(): lax.all_to_all(parts, 'stream', split_axis=0, concat_axis=0, tiled=True)]
    all_to_all x12 -> x0, waiting for transfers between devices: 106 us -> none  [the longest x8 63.2 us: block_x(): lax.all_to_all(along_x(matrix, lax.all_to_all(fields, 'stream', split_axi...]
    dot_general x18 -> x0, matrix products: 62.3 us -> none  [the longest x9 43.2 us: along_x(): jnp.einsum('ij,fjyz->fiyz', matrix, fields, precision=lax.Precision.HIGHEST)]
    all_to_all x12 -> x0, starting transfers between devices: 54.5 us -> none  [the longest x8 35.6 us: block_x(): lax.all_to_all(along_x(matrix, lax.all_to_all(fields, 'stream', split_axi...]
    pallas_call x0 -> x9, Pallas kernels: none -> 43.1 us  [row_call(): pl.pallas_call(kernel, grid=(rows,), in_specs=[block, pl.BlockSpec((nx, n...]
    transpose x9 -> x1, local copies, waits for them, and re-layouts: 26.9 us -> 0.24 us  [shards(): fields = parts.transpose(1, 2, 0, 3, 4).reshape(rows, count, nx, nz)]
    all_to_all x17 -> x0, local copies, waits for them, and re-layouts: 26 us -> none  [the longest x8 18.1 us: block_x(): lax.all_to_all(along_x(matrix, lax.all_to_all(fields, 'stream', split_axi...]
    ppermute x36 -> x28, starting transfers between devices: 102 us -> 78.3 us  [the longest x24 70.4 us: shift(): return lax.ppermute(part, axes, pairs)]
  transfers between devices with their start and end apart: 48 -> 28, of which waited for: 28 -> 17; matrix products, arithmetic and copies ran while one was open for 16% -> 10% of each run, Pallas kernels for 0% -> 13%
where the time goes in v1:
time: 293 us; the launch traced here: 291 us
  starting transfers between devices  78.3 us (27%)
  blocking collectives  49 us (17%)
  Pallas kernels  43.1 us (15%)
  other arithmetic  42.3 us (14%)
  waiting for transfers between devices  42.3 us (14%)
  local copies, waits for them, and re-layouts  35.4 us (12%)
    ppermute x24, starting transfers between devices, shift(): return lax.ppermute(part, axes, pairs)  70.4 us
    all_to_all x2, blocking collectives, shards(): lax.all_to_all(parts, 'stream', split_axis=0, concat_axis=0, tiled=True)  49 us
    pallas_call x9, Pallas kernels, row_call(): pl.pallas_call(kernel, grid=(rows,), in_specs=[block, pl.BlockSpec((nx, n...  43.1 us
    ppermute x24, waiting for transfers between devices, shift(): return lax.ppermute(part, axes, pairs)  42.3 us
    unnamed x41, local copies, waits for them, and re-layouts  17.2 us
    another operation x6, local copies, waits for them, and re-layouts, shards(): jnp.stack([part[:, 0] - time_step * dy[:, 1], part[:, 1] + time_step * fo...  8.77 us
    ppermute x4, starting transfers between devices, shards(): forcing = lax.ppermute(source, 'section', [(0, 1)])  7.9 us
    concatenate x8, other arithmetic, shards(): near = jnp.concatenate([before, pv, after], axis=0)  7.83 us
  transfers between devices with their start and end apart: 28, of which 17 were waited for; matrix products, arithmetic and copies ran while one was open for 10% of the time, Pallas kernels for 13%

profile of v1, /device:TPU:16, one launch (start us, length us, event | category | flops | bytes accessed | tf_op | source)
XLA Modules:
  0.0 291.2 jit_solution(15321466677755402772)
XLA Ops:
  0.0 2.2 copy.158
  2.8 28.9 %all_to_all.10 = f32[4,4,4,64,128]{4,3,1,2,0:T(8,128)S(1)} all-to-all(f32[4,4,4,64,128]{4,3,1,2,0:T(8,128)S(1)} %copy.159), channel_id=1, replica_groups=mesh['section'=2,'stream'=4,'slab'=4] {'stream'}, dimensions={0} | all-to-all | bytes 4194304 | tf_op jit(solution)/shard_map/all_to_all | solution.py:141
  34.4 2.3 collective-permute-start.2
  36.7 3.5 %collective-permute-start.3 = (f32[1,2,256,128]{3,2,0,1:T(8,128)}, f32[1,2,256,128]{3,2,0,1:T(8,128)}, u32[]{:S(2)}, u32[]{:S(2)}) collective-permute-start(f32[1,2,256,128]{3,2,0,1:T(8,128)} %get-tuple-element.102), channel_id=1, source_target_pairs={{0,4},{4,12},{12,8},{8,9},{9,13},{13,5},{5,1},{1,2},{2,6},{6,14},{... | collective-permute-start | bytes 786440 | tf_op jit(solution)/shard_map/ppermute | solution.py:98
  40.4 2.4 collective-permute-done.2
  42.8 2.5 collective-permute-done.3
  48.9 2.6 collective-permute-start.4
  52.5 2.8 collective-permute-start
  55.3 3.0 %collective-permute-start.1 = (f32[2,2,256,128]{3,2,0,1:T(8,128)}, f32[2,2,256,128]{3,2,0,1:T(8,128)}, u32[]{:S(2)}, u32[]{:S(2)}) collective-permute-start(f32[2,2,256,128]{3,2,0,1:T(8,128)} %get-tuple-element.100), channel_id=1, source_target_pairs={{0,4},{4,12},{12,8},{8,9},{9,13},{13,5},{5,1},{1,2},{2,6},{6,14},{... | collective-permute-start | bytes 1572872 | tf_op jit(solution)/shard_map/ppermute | solution.py:98
  60.6 4.8 %shard_map.69 = f32[4,4,256,128]{3,2,1,0:T(8,128)} custom-call(f32[4,4,256,128]{3,2,1,0:T(8,128)} %copy.162.fields_ref, f32[256,256]{1,0:T(8,128)} %dx_ref.15, f32[128,128]{1,0:T(8,128)} %bitcast.374), custom_call_target="tpu_custom_call" | custom-call | flops 1207959552 | bytes 4194304 | tf_op jit(solution)/shard_map/pallas_call | solution.py:63
  65.3 2.0 collective-permute-done.1
  72.3 2.5 collective-permute-start.5
  74.8 3.4 %collective-permute-start.6 = (f32[2,2,256,128]{3,2,0,1:T(8,128)S(1)}, f32[2,2,256,128]{3,2,0,1:T(8,128)S(1)}, u32[]{:S(2)}, u32[]{:S(2)}) collective-permute-start(f32[2,2,256,128]{3,2,0,1:T(8,128)S(1)} %get-tuple-element.96), channel_id=1, source_target_pairs={{0,4},{4,12},{12,8},{8,9},{9,13},{13,5},{5,1},{1,2},{2,6},{6,14},{... | collective-permute-start | bytes 1572872 | tf_op jit(solution)/shard_map/ppermute | solution.py:98
  79.8 4.8 %shard_map.70 = f32[4,4,256,128]{3,2,1,0:T(8,128)} custom-call(f32[4,4,256,128]{3,2,1,0:T(8,128)} %copy.172.fields_ref, f32[256,256]{1,0:T(8,128)} %dx_ref.15, f32[128,128]{1,0:T(8,128)} %bitcast.375), custom_call_target="tpu_custom_call" | custom-call | flops 1207959552 | bytes 4194304 | tf_op jit(solution)/shard_map/pallas_call | solution.py:63
  89.6 3.4 %collective-permute-start.9 = (f32[1,2,256,128]{3,2,0,1:T(8,128)S(1)}, f32[1,2,256,128]{3,2,0,1:T(8,128)S(1)}, u32[]{:S(2)}, u32[]{:S(2)}) collective-permute-start(f32[1,2,256,128]{3,2,0,1:T(8,128)S(1)} %get-tuple-element.91), channel_id=1, source_target_pairs={{4,0},{12,4},{8,12},{9,8},{13,9},{5,13},{1,5},{2,1},{6,2},{14,6},{... | collective-permute-start | bytes 786440 | tf_op jit(solution)/shard_map/ppermute | solution.py:98
  92.9 2.5 collective-permute-start.10
  95.4 2.4 collective-permute-done.9
  97.8 3.4 %collective-permute-done.10 = f32[1,2,256,128]{3,2,0,1:T(8,128)S(1)} collective-permute-done((f32[1,2,256,128]{3,2,0,1:T(8,128)S(1)}, f32[1,2,256,128]{3,2,0,1:T(8,128)S(1)}, u32[]{:S(2)}, u32[]{:S(2)}) %collective-permute-start.10) | collective-permute-done | bytes 262176 | tf_op jit(solution)/shard_map/ppermute | solution.py:98
  106.3 2.3 collective-permute-start.7
  108.6 3.5 %collective-permute-start.8 = (f32[2,2,256,128]{3,2,0,1:T(8,128)}, f32[2,2,256,128]{3,2,0,1:T(8,128)}, u32[]{:S(2)}, u32[]{:S(2)}) collective-permute-start(f32[2,2,256,128]{3,2,0,1:T(8,128)} %get-tuple-element.90), channel_id=1, source_target_pairs={{0,4},{4,12},{12,8},{8,9},{9,13},{13,5},{5,1},{1,2},{2,6},{6,14},{... | collective-permute-start | bytes 1572872 | tf_op jit(solution)/shard_map/ppermute | solution.py:98
  113.8 4.8 %shard_map.71 = f32[4,4,256,128]{3,2,1,0:T(8,128)} custom-call(f32[4,4,256,128]{3,2,1,0:T(8,128)} %copy.180.fields_ref, f32[256,256]{1,0:T(8,128)} %dx_ref.15, f32[128,128]{1,0:T(8,128)} %bitcast.376), custom_call_target="tpu_custom_call" | custom-call | flops 1207959552 | bytes 4194304 | tf_op jit(solution)/shard_map/pallas_call | solution.py:63
  120.3 2.8 collective-permute-done.8
  127.4 2.5 collective-permute-start.12
  129.9 3.5 %collective-permute-start.13 = (f32[2,2,256,128]{3,2,0,1:T(8,128)}, f32[2,2,256,128]{3,2,0,1:T(8,128)}, u32[]{:S(2)}, u32[]{:S(2)}) collective-permute-start(f32[2,2,256,128]{3,2,0,1:T(8,128)} %get-tuple-element.86), channel_id=1, source_target_pairs={{0,4},{4,12},{12,8},{8,9},{9,13},{13,5},{5,1},{1,2},{2,6},{6,14},{... | collective-permute-start | bytes 1572872 | tf_op jit(solution)/shard_map/ppermute | solution.py:98
  135.1 4.8 %shard_map.72 = f32[4,4,256,128]{3,2,1,0:T(8,128)} custom-call(f32[4,4,256,128]{3,2,1,0:T(8,128)} %copy.190.fields_ref, f32[256,256]{1,0:T(8,128)} %dx_ref.15, f32[128,128]{1,0:T(8,128)} %bitcast.377), custom_call_target="tpu_custom_call" | custom-call | flops 1207959552 | bytes 4194304 | tf_op jit(solution)/shard_map/pallas_call | solution.py:63
  144.7 3.4 %collective-permute-start.16 = (f32[1,2,256,128]{3,2,0,1:T(8,128)S(1)}, f32[1,2,256,128]{3,2,0,1:T(8,128)S(1)}, u32[]{:S(2)}, u32[]{:S(2)}) collective-permute-start(f32[1,2,256,128]{3,2,0,1:T(8,128)S(1)} %get-tuple-element.81), channel_id=1, source_target_pairs={{4,0},{12,4},{8,12},{9,8},{13,9},{5,13},{1,5},{2,1},{6,2},{14,6},{... | collective-permute-start | bytes 786440 | tf_op jit(solution)/shard_map/ppermute | solution.py:98
  148.0 2.5 collective-permute-start.17
  150.5 2.4 collective-permute-done.16
  152.9 3.4 %collective-permute-done.17 = f32[1,2,256,128]{3,2,0,1:T(8,128)S(1)} collective-permute-done((f32[1,2,256,128]{3,2,0,1:T(8,128)S(1)}, f32[1,2,256,128]{3,2,0,1:T(8,128)S(1)}, u32[]{:S(2)}, u32[]{:S(2)}) %collective-permute-start.17) | collective-permute-done | bytes 262176 | tf_op jit(solution)/shard_map/ppermute | solution.py:98
  161.4 3.4 %collective-permute-start.14 = (f32[2,2,256,128]{3,2,0,1:T(8,128)}, f32[2,2,256,128]{3,2,0,1:T(8,128)S(1)}, u32[]{:S(2)}, u32[]{:S(2)}) collective-permute-start(f32[2,2,256,128]{3,2,0,1:T(8,128)} %get-tuple-element.79), channel_id=1, source_target_pairs={{4,0},{12,4},{8,12},{9,8},{13,9},{5,13},{1,5},{2,1},{6,2},{14,6},{... | collective-permute-start | bytes 1572872 | tf_op jit(solution)/shard_map/ppermute | solution.py:98
  164.7 2.5 collective-permute-start.15
  168.9 4.8 %shard_map.73 = f32[4,4,256,128]{3,2,1,0:T(8,128)} custom-call(f32[4,4,256,128]{3,2,1,0:T(8,128)} %copy.198.fields_ref, f32[256,256]{1,0:T(8,128)} %dx_ref.15, f32[128,128]{1,0:T(8,128)} %bitcast.378), custom_call_target="tpu_custom_call" | custom-call | flops 1207959552 | bytes 4194304 | tf_op jit(solution)/shard_map/pallas_call | solution.py:63
  173.6 2.1 collective-permute-done.14
  175.8 3.8 %collective-permute-done.15 = f32[2,2,256,128]{3,2,0,1:T(8,128)} collective-permute-done((f32[2,2,256,128]{3,2,0,1:T(8,128)}, f32[2,2,256,128]{3,2,0,1:T(8,128)}, u32[]{:S(2)}, u32[]{:S(2)}) %collective-permute-start.15) | collective-permute-done | bytes 524320 | tf_op jit(solution)/shard_map/ppermute | solution.py:98
  185.7 3.9 %collective-permute-start.20 = (f32[2,2,256,128]{3,2,0,1:T(8,128)S(1)}, f32[2,2,256,128]{3,2,0,1:T(8,128)S(1)}, u32[]{:S(2)}, u32[]{:S(2)}) collective-permute-start(f32[2,2,256,128]{3,2,0,1:T(8,128)S(1)} %get-tuple-element.76), channel_id=1, source_target_pairs={{0,4},{4,12},{12,8},{8,9},{9,13},{13,5},{5,1},{1,2},{2,6},{6,14},{... | collective-permute-start | bytes 1572872 | tf_op jit(solution)/shard_map/ppermute | solution.py:98
  191.3 4.8 %shard_map.74 = f32[4,4,256,128]{3,2,1,0:T(8,128)} custom-call(f32[4,4,256,128]{3,2,1,0:T(8,128)} %copy.208.fields_ref, f32[256,256]{1,0:T(8,128)} %dx_ref.15, f32[128,128]{1,0:T(8,128)} %bitcast.379), custom_call_target="tpu_custom_call" | custom-call | flops 1207959552 | bytes 4194304 | tf_op jit(solution)/shard_map/pallas_call | solution.py:63
  201.3 3.9 %collective-permute-start.24 = (f32[1,2,256,128]{3,2,0,1:T(8,128)S(1)}, f32[1,2,256,128]{3,2,0,1:T(8,128)S(1)}, u32[]{:S(2)}, u32[]{:S(2)}) collective-permute-start(f32[1,2,256,128]{3,2,0,1:T(8,128)S(1)} %get-tuple-element.72), channel_id=1, source_target_pairs={{0,4},{4,12},{12,8},{8,9},{9,13},{13,5},{5,1},{1,2},{2,6},{6,14},{... | collective-permute-start | bytes 786440 | tf_op jit(solution)/shard_map/ppermute | solution.py:98
  205.3 2.3 collective-permute-done.23
  212.2 2.6 collective-permute-start.25
  217.7 3.9 %collective-permute-start.22 = (f32[2,2,256,128]{3,2,0,1:T(8,128)}, f32[2,2,256,128]{3,2,0,1:T(8,128)S(1)}, u32[]{:S(2)}, u32[]{:S(2)}) collective-permute-start(f32[2,2,256,128]{3,2,0,1:T(8,128)} %get-tuple-element.70), channel_id=1, source_target_pairs={{0,4},{4,12},{12,8},{8,9},{9,13},{13,5},{5,1},{1,2},{2,6},{6,14},{... | collective-permute-start | bytes 1572872 | tf_op jit(solution)/shard_map/ppermute | solution.py:98
  224.0 4.8 %shard_map.75 = f32[4,4,256,128]{3,2,1,0:T(8,128)} custom-call(f32[4,4,256,128]{3,2,1,0:T(8,128)} %copy.217.fields_ref, f32[256,256]{1,0:T(8,128)} %dx_ref.15, f32[128,128]{1,0:T(8,128)} %bitcast.380), custom_call_target="tpu_custom_call" | custom-call | flops 1207959552 | bytes 4194304 | tf_op jit(solution)/shard_map/pallas_call | solution.py:63
  228.8 5.8 %collective-permute-done.22 = f32[2,2,256,128]{3,2,0,1:T(8,128)S(1)} collective-permute-done((f32[2,2,256,128]{3,2,0,1:T(8,128)}, f32[2,2,256,128]{3,2,0,1:T(8,128)S(1)}, u32[]{:S(2)}, u32[]{:S(2)}) %collective-permute-start.22) | collective-permute-done | bytes 524320 | tf_op jit(solution)/shard_map/ppermute | solution.py:98
  238.2 3.9 %collective-permute-start.27 = (f32[2,2,256,128]{3,2,1,0:T(8,128)S(1)}, f32[2,2,256,128]{3,2,1,0:T(8,128)}, u32[]{:S(2)}, u32[]{:S(2)}) collective-permute-start(f32[2,2,256,128]{3,2,1,0:T(8,128)S(1)} %fusion.61), channel_id=1, source_target_pairs={{0,4},{4,12},{12,8},{8,9},{9,13},{13,5},{5,1},{1,2},{2,6},{6,14},{... | collective-permute-start | bytes 1572872 | tf_op jit(solution)/shard_map/ppermute | solution.py:98
  243.0 2.1 collective-permute-start.26
  247.8 4.8 %shard_map.76 = f32[4,4,256,128]{3,2,1,0:T(8,128)} custom-call(f32[4,4,256,128]{3,2,1,0:T(8,128)} %pad_maximum_fusion.6.fields_ref, f32[256,256]{1,0:T(8,128)} %dx_ref.15, f32[128,128]{1,0:T(8,128)} %bitcast.381), custom_call_target="tpu_custom_call" | custom-call | flops 1207959552 | bytes 4194304 | tf_op jit(solution)/shard_map/pallas_call | solution.py:63
  260.8 5.0 %shard_map.77 = f32[4,4,256,128]{3,2,1,0:T(8,128)} custom-call(f32[4,4,256,128]{3,2,1,0:T(8,128)} %pad_maximum_fusion.7.fields_ref, f32[256,256]{1,0:T(8,128)} %fx_ref.1, f32[128,128]{1,0:T(8,128)} %bitcast.382), custom_call_target="tpu_custom_call" | custom-call | flops 1207959552 | bytes 4194304 | tf_op jit(solution)/shard_map/pallas_call | solution.py:63
  267.5 20.1 %all_to_all.11 = f32[4,4,4,64,128]{4,3,1,2,0:T(8,128)S(1)} all-to-all(f32[4,4,4,64,128]{4,3,1,2,0:T(8,128)S(1)} %bitcast.373), channel_id=1, replica_groups=mesh['section'=2,'stream'=4,'slab'=4] {'stream'}, dimensions={0} | all-to-all | bytes 4194304 | tf_op jit(solution)/shard_map/all_to_all | solution.py:175
  288.6 2.5 copy.241
  (148 shorter events, 88.4 us)
Async XLA Ops:
  33.5 6.7 %copy-start.17 = (s32[16,1]{0,1:T(1,128)S(1)}, s32[16,1]{0,1:T(1,128)}, u32[]{:S(2)}) copy-start(s32[16,1]{0,1:T(1,128)} %param.7) | copy-start | bytes 196
  34.4 8.5 %collective-permute-start.2 = (f32[1,2,256,128]{3,2,0,1:T(8,128)}, f32[1,2,256,128]{3,2,0,1:T(8,128)S(1)}, u32[]{:S(2)}, u32[]{:S(2)}) collective-permute-start(f32[1,2,256,128]{3,2,0,1:T(8,128)} %get-tuple-element.101), channel_id=1, source_target_pairs={{4,0},{12,4},{8,12},{9,8},{13,9},{5,13},{1,5},{2,1},{6,2},{14,6},{... | collective-permute-start | bytes 786440 | tf_op jit(solution)/shard_map/ppermute | solution.py:98
  36.7 8.6 %collective-permute-start.3 = (f32[1,2,256,128]{3,2,0,1:T(8,128)}, f32[1,2,256,128]{3,2,0,1:T(8,128)}, u32[]{:S(2)}, u32[]{:S(2)}) collective-permute-start(f32[1,2,256,128]{3,2,0,1:T(8,128)} %get-tuple-element.102), channel_id=1, source_target_pairs={{0,4},{4,12},{12,8},{8,9},{9,13},{13,5},{5,1},{1,2},{2,6},{6,14},{... | collective-permute-start | bytes 786440 | tf_op jit(solution)/shard_map/ppermute | solution.py:98
  40.4 6.0 %copy-start.12 = (f32[4,256,128]{2,1,0:T(8,128)S(1)}, f32[4,256,128]{2,1,0:T(8,128)}, u32[]{:S(2)}) copy-start(f32[4,256,128]{2,1,0:T(8,128)} %get-tuple-element.57) | copy-start | bytes 1572868
  40.4 6.0 %copy-start.13 = (f32[4,256,128]{2,1,0:T(8,128)S(1)}, f32[4,256,128]{2,1,0:T(8,128)}, u32[]{:S(2)}) copy-start(f32[4,256,128]{2,1,0:T(8,128)} %get-tuple-element.58) | copy-start | bytes 1572868
  40.4 6.0 %copy-start.14 = (f32[4,256,128]{2,1,0:T(8,128)S(1)}, f32[4,256,128]{2,1,0:T(8,128)}, u32[]{:S(2)}) copy-start(f32[4,256,128]{2,1,0:T(8,128)} %get-tuple-element.59) | copy-start | bytes 1572868
  47.5 4.0 %copy-start.10 = (f32[4,1,256,128]{3,2,0,1:T(8,128)S(1)}, f32[4,1,256,128]{3,2,0,1:T(8,128)}, u32[]{:S(2)}) copy-start(f32[4,1,256,128]{3,2,0,1:T(8,128)} %get-tuple-element.56) | copy-start | bytes 1572868
  47.5 4.0 %copy-start.11 = (f32[4,1,256,128]{3,2,0,1:T(8,128)S(1)}, f32[4,1,256,128]{3,2,0,1:T(8,128)}, u32[]{:S(2)}) copy-start(f32[4,1,256,128]{3,2,0,1:T(8,128)} %get-tuple-element.62) | copy-start | bytes 1572868
  48.9 9.5 %copy-start.15 = (f32[128,128]{1,0:T(8,128)S(1)}, f32[128,128]{1,0:T(8,128)}, u32[]{:S(2)}) copy-start(f32[128,128]{1,0:T(8,128)} %param.9) | copy-start | bytes 196612
  48.9 20.2 %collective-permute-start.4 = (f32[4,3,256,128]{3,2,0,1:T(8,128)}, f32[4,3,256,128]{3,2,0,1:T(8,128)}, u32[]{:S(2)}, u32[]{:S(2)}) collective-permute-start(f32[4,3,256,128]{3,2,0,1:T(8,128)} %maximum_multiply_fusion), channel_id=1, source_target_pairs={{0,16},{1,17},{2,18},{3,19},{4,20},{5,21},{6,22},{7,23},{8,24},{9,... | collective-permute-start | bytes 4718600 | tf_op jit(solution)/shard_map/ppermute | solution.py:159
  52.5 12.8 %collective-permute-start = (f32[2,2,256,128]{3,2,0,1:T(8,128)}, f32[2,2,256,128]{3,2,0,1:T(8,128)}, u32[]{:S(2)}, u32[]{:S(2)}) collective-permute-start(f32[2,2,256,128]{3,2,0,1:T(8,128)} %get-tuple-element.99), channel_id=1, source_target_pairs={{4,0},{12,4},{8,12},{9,8},{13,9},{5,13},{1,5},{2,1},{6,2},{14,6},{... | collective-permute-start | bytes 1572872 | tf_op jit(solution)/shard_map/ppermute | solution.py:98
  55.3 12.0 %collective-permute-start.1 = (f32[2,2,256,128]{3,2,0,1:T(8,128)}, f32[2,2,256,128]{3,2,0,1:T(8,128)}, u32[]{:S(2)}, u32[]{:S(2)}) collective-permute-start(f32[2,2,256,128]{3,2,0,1:T(8,128)} %get-tuple-element.100), channel_id=1, source_target_pairs={{0,4},{4,12},{12,8},{8,9},{9,13},{13,5},{5,1},{1,2},{2,6},{6,14},{... | collective-permute-start | bytes 1572872 | tf_op jit(solution)/shard_map/ppermute | solution.py:98
  68.9 1.6 copy-start.3
  72.3 12.3 %collective-permute-start.5 = (f32[2,2,256,128]{3,2,0,1:T(8,128)S(1)}, f32[2,2,256,128]{3,2,0,1:T(8,128)S(1)}, u32[]{:S(2)}, u32[]{:S(2)}) collective-permute-start(f32[2,2,256,128]{3,2,0,1:T(8,128)S(1)} %get-tuple-element.95), channel_id=1, source_target_pairs={{4,0},{12,4},{8,12},{9,8},{13,9},{5,13},{1,5},{2,1},{6,2},{14,6},{... | collective-permute-start | bytes 1572872 | tf_op jit(solution)/shard_map/ppermute | solution.py:98
  74.8 11.1 %collective-permute-start.6 = (f32[2,2,256,128]{3,2,0,1:T(8,128)S(1)}, f32[2,2,256,128]{3,2,0,1:T(8,128)S(1)}, u32[]{:S(2)}, u32[]{:S(2)}) collective-permute-start(f32[2,2,256,128]{3,2,0,1:T(8,128)S(1)} %get-tuple-element.96), channel_id=1, source_target_pairs={{0,4},{4,12},{12,8},{8,9},{9,13},{13,5},{5,1},{1,2},{2,6},{6,14},{... | collective-permute-start | bytes 1572872 | tf_op jit(solution)/shard_map/ppermute | solution.py:98
  86.2 1.6 copy-start.6
  89.6 8.3 %collective-permute-start.9 = (f32[1,2,256,128]{3,2,0,1:T(8,128)S(1)}, f32[1,2,256,128]{3,2,0,1:T(8,128)S(1)}, u32[]{:S(2)}, u32[]{:S(2)}) collective-permute-start(f32[1,2,256,128]{3,2,0,1:T(8,128)S(1)} %get-tuple-element.91), channel_id=1, source_target_pairs={{4,0},{12,4},{8,12},{9,8},{13,9},{5,13},{1,5},{2,1},{6,2},{14,6},{... | collective-permute-start | bytes 786440 | tf_op jit(solution)/shard_map/ppermute | solution.py:98
  92.9 8.3 %collective-permute-start.10 = (f32[1,2,256,128]{3,2,0,1:T(8,128)S(1)}, f32[1,2,256,128]{3,2,0,1:T(8,128)S(1)}, u32[]{:S(2)}, u32[]{:S(2)}) collective-permute-start(f32[1,2,256,128]{3,2,0,1:T(8,128)S(1)} %get-tuple-element.92), channel_id=1, source_target_pairs={{0,4},{4,12},{12,8},{8,9},{9,13},{13,5},{5,1},{1,2},{2,6},{6,14},{... | collective-permute-start | bytes 786440 | tf_op jit(solution)/shard_map/ppermute | solution.py:98
  103.8 20.8 %collective-permute-start.11 = (f32[4,3,256,128]{3,2,0,1:T(8,128)}, f32[4,3,256,128]{3,2,0,1:T(8,128)S(1)}, u32[]{:S(2)}, u32[]{:S(2)}) collective-permute-start(f32[4,3,256,128]{3,2,0,1:T(8,128)} %maximum_multiply_fusion.1), channel_id=1, source_target_pairs={{0,16},{1,17},{2,18},{3,19},{4,20},{5,21},{6,22},{7,23},{8,24},{9,... | collective-permute-start | bytes 4718600 | tf_op jit(solution)/shard_map/ppermute | solution.py:159
  106.3 14.0 %collective-permute-start.7 = (f32[2,2,256,128]{3,2,0,1:T(8,128)}, f32[2,2,256,128]{3,2,0,1:T(8,128)S(1)}, u32[]{:S(2)}, u32[]{:S(2)}) collective-permute-start(f32[2,2,256,128]{3,2,0,1:T(8,128)} %get-tuple-element.89), channel_id=1, source_target_pairs={{4,0},{12,4},{8,12},{9,8},{13,9},{5,13},{1,5},{2,1},{6,2},{14,6},{... | collective-permute-start | bytes 1572872 | tf_op jit(solution)/shard_map/ppermute | solution.py:98
  108.6 14.4 %collective-permute-start.8 = (f32[2,2,256,128]{3,2,0,1:T(8,128)}, f32[2,2,256,128]{3,2,0,1:T(8,128)}, u32[]{:S(2)}, u32[]{:S(2)}) collective-permute-start(f32[2,2,256,128]{3,2,0,1:T(8,128)} %get-tuple-element.90), channel_id=1, source_target_pairs={{0,4},{4,12},{12,8},{8,9},{9,13},{13,5},{5,1},{1,2},{2,6},{6,14},{... | collective-permute-start | bytes 1572872 | tf_op jit(solution)/shard_map/ppermute | solution.py:98
  124.4 1.6 copy-start.4
  127.4 12.5 %collective-permute-start.12 = (f32[2,2,256,128]{3,2,0,1:T(8,128)}, f32[2,2,256,128]{3,2,0,1:T(8,128)S(1)}, u32[]{:S(2)}, u32[]{:S(2)}) collective-permute-start(f32[2,2,256,128]{3,2,0,1:T(8,128)} %get-tuple-element.85), channel_id=1, source_target_pairs={{4,0},{12,4},{8,12},{9,8},{13,9},{5,13},{1,5},{2,1},{6,2},{14,6},{... | collective-permute-start | bytes 1572872 | tf_op jit(solution)/shard_map/ppermute | solution.py:98
  129.9 11.4 %collective-permute-start.13 = (f32[2,2,256,128]{3,2,0,1:T(8,128)}, f32[2,2,256,128]{3,2,0,1:T(8,128)}, u32[]{:S(2)}, u32[]{:S(2)}) collective-permute-start(f32[2,2,256,128]{3,2,0,1:T(8,128)} %get-tuple-element.86), channel_id=1, source_target_pairs={{0,4},{4,12},{12,8},{8,9},{9,13},{13,5},{5,1},{1,2},{2,6},{6,14},{... | collective-permute-start | bytes 1572872 | tf_op jit(solution)/shard_map/ppermute | solution.py:98
  142.7 1.6 copy-start.7
  144.7 8.3 %collective-permute-start.16 = (f32[1,2,256,128]{3,2,0,1:T(8,128)S(1)}, f32[1,2,256,128]{3,2,0,1:T(8,128)S(1)}, u32[]{:S(2)}, u32[]{:S(2)}) collective-permute-start(f32[1,2,256,128]{3,2,0,1:T(8,128)S(1)} %get-tuple-element.81), channel_id=1, source_target_pairs={{4,0},{12,4},{8,12},{9,8},{13,9},{5,13},{1,5},{2,1},{6,2},{14,6},{... | collective-permute-start | bytes 786440 | tf_op jit(solution)/shard_map/ppermute | solution.py:98
  148.0 8.3 %collective-permute-start.17 = (f32[1,2,256,128]{3,2,0,1:T(8,128)S(1)}, f32[1,2,256,128]{3,2,0,1:T(8,128)S(1)}, u32[]{:S(2)}, u32[]{:S(2)}) collective-permute-start(f32[1,2,256,128]{3,2,0,1:T(8,128)S(1)} %get-tuple-element.82), channel_id=1, source_target_pairs={{0,4},{4,12},{12,8},{8,9},{9,13},{13,5},{5,1},{1,2},{2,6},{6,14},{... | collective-permute-start | bytes 786440 | tf_op jit(solution)/shard_map/ppermute | solution.py:98
  158.9 22.2 %collective-permute-start.18 = (f32[4,3,256,128]{3,2,0,1:T(8,128)}, f32[4,3,256,128]{3,2,0,1:T(8,128)S(1)}, u32[]{:S(2)}, u32[]{:S(2)}) collective-permute-start(f32[4,3,256,128]{3,2,0,1:T(8,128)} %maximum_multiply_fusion.2), channel_id=1, source_target_pairs={{0,16},{1,17},{2,18},{3,19},{4,20},{5,21},{6,22},{7,23},{8,24},{9,... | collective-permute-start | bytes 4718600 | tf_op jit(solution)/shard_map/ppermute | solution.py:159
  161.4 14.4 %collective-permute-start.14 = (f32[2,2,256,128]{3,2,0,1:T(8,128)}, f32[2,2,256,128]{3,2,0,1:T(8,128)S(1)}, u32[]{:S(2)}, u32[]{:S(2)}) collective-permute-start(f32[2,2,256,128]{3,2,0,1:T(8,128)} %get-tuple-element.79), channel_id=1, source_target_pairs={{4,0},{12,4},{8,12},{9,8},{13,9},{5,13},{1,5},{2,1},{6,2},{14,6},{... | collective-permute-start | bytes 1572872 | tf_op jit(solution)/shard_map/ppermute | solution.py:98
  164.7 14.8 %collective-permute-start.15 = (f32[2,2,256,128]{3,2,0,1:T(8,128)}, f32[2,2,256,128]{3,2,0,1:T(8,128)}, u32[]{:S(2)}, u32[]{:S(2)}) collective-permute-start(f32[2,2,256,128]{3,2,0,1:T(8,128)} %get-tuple-element.80), channel_id=1, source_target_pairs={{0,4},{4,12},{12,8},{8,9},{9,13},{13,5},{5,1},{1,2},{2,6},{6,14},{... | collective-permute-start | bytes 1572872 | tf_op jit(solution)/shard_map/ppermute | solution.py:98
  180.9 1.6 copy-start.5
  182.5 1.2 copy-start.8
  183.7 12.3 %collective-permute-start.19 = (f32[2,2,256,128]{3,2,0,1:T(8,128)S(1)}, f32[2,2,256,128]{3,2,0,1:T(8,128)S(1)}, u32[]{:S(2)}, u32[]{:S(2)}) collective-permute-start(f32[2,2,256,128]{3,2,0,1:T(8,128)S(1)} %get-tuple-element.75), channel_id=1, source_target_pairs={{4,0},{12,4},{8,12},{9,8},{13,9},{5,13},{1,5},{2,1},{6,2},{14,6},{... | collective-permute-start | bytes 1572872 | tf_op jit(solution)/shard_map/ppermute | solution.py:98
  185.7 11.1 %collective-permute-start.20 = (f32[2,2,256,128]{3,2,0,1:T(8,128)S(1)}, f32[2,2,256,128]{3,2,0,1:T(8,128)S(1)}, u32[]{:S(2)}, u32[]{:S(2)}) collective-permute-start(f32[2,2,256,128]{3,2,0,1:T(8,128)S(1)} %get-tuple-element.76), channel_id=1, source_target_pairs={{0,4},{4,12},{12,8},{8,9},{9,13},{13,5},{5,1},{1,2},{2,6},{6,14},{... | collective-permute-start | bytes 1572872 | tf_op jit(solution)/shard_map/ppermute | solution.py:98
  197.1 1.6 copy-start.1
  197.1 2.0 copy-start.9
  199.4 8.3 %collective-permute-start.23 = (f32[1,2,256,128]{3,2,0,1:T(8,128)S(1)}, f32[1,2,256,128]{3,2,0,1:T(8,128)S(1)}, u32[]{:S(2)}, u32[]{:S(2)}) collective-permute-start(f32[1,2,256,128]{3,2,0,1:T(8,128)S(1)} %get-tuple-element.71), channel_id=1, source_target_pairs={{4,0},{12,4},{8,12},{9,8},{13,9},{5,13},{1,5},{2,1},{6,2},{14,6},{... | collective-permute-start | bytes 786440 | tf_op jit(solution)/shard_map/ppermute | solution.py:98
  201.3 8.3 %collective-permute-start.24 = (f32[1,2,256,128]{3,2,0,1:T(8,128)S(1)}, f32[1,2,256,128]{3,2,0,1:T(8,128)S(1)}, u32[]{:S(2)}, u32[]{:S(2)}) collective-permute-start(f32[1,2,256,128]{3,2,0,1:T(8,128)S(1)} %get-tuple-element.72), channel_id=1, source_target_pairs={{0,4},{4,12},{12,8},{8,9},{9,13},{13,5},{5,1},{1,2},{2,6},{6,14},{... | collective-permute-start | bytes 786440 | tf_op jit(solution)/shard_map/ppermute | solution.py:98
  212.2 9.5 %copy-start.16 = (f32[128,128]{1,0:T(8,128)S(1)}, f32[128,128]{1,0:T(8,128)}, u32[]{:S(2)}) copy-start(f32[128,128]{1,0:T(8,128)} %param.11) | copy-start | bytes 196612
  212.2 23.0 %collective-permute-start.25 = (f32[4,3,256,128]{3,2,0,1:T(8,128)}, f32[4,3,256,128]{3,2,0,1:T(8,128)}, u32[]{:S(2)}, u32[]{:S(2)}) collective-permute-start(f32[4,3,256,128]{3,2,0,1:T(8,128)} %maximum_multiply_fusion.3), channel_id=1, source_target_pairs={{0,16},{1,17},{2,18},{3,19},{4,20},{5,21},{6,22},{7,23},{8,24},{9,... | collective-permute-start | bytes 4718600 | tf_op jit(solution)/shard_map/ppermute | solution.py:159
  215.8 13.0 %collective-permute-start.21 = (f32[2,2,256,128]{3,2,0,1:T(8,128)}, f32[2,2,256,128]{3,2,0,1:T(8,128)S(1)}, u32[]{:S(2)}, u32[]{:S(2)}) collective-permute-start(f32[2,2,256,128]{3,2,0,1:T(8,128)} %get-tuple-element.69), channel_id=1, source_target_pairs={{4,0},{12,4},{8,12},{9,8},{13,9},{5,13},{1,5},{2,1},{6,2},{14,6},{... | collective-permute-start | bytes 1572872 | tf_op jit(solution)/shard_map/ppermute | solution.py:98
  217.7 16.9 %collective-permute-start.22 = (f32[2,2,256,128]{3,2,0,1:T(8,128)}, f32[2,2,256,128]{3,2,0,1:T(8,128)S(1)}, u32[]{:S(2)}, u32[]{:S(2)}) collective-permute-start(f32[2,2,256,128]{3,2,0,1:T(8,128)} %get-tuple-element.70), channel_id=1, source_target_pairs={{0,4},{4,12},{12,8},{8,9},{9,13},{13,5},{5,1},{1,2},{2,6},{6,14},{... | collective-permute-start | bytes 1572872 | tf_op jit(solution)/shard_map/ppermute | solution.py:98
  235.0 1.6 copy-start
  238.2 15.7 %collective-permute-start.27 = (f32[2,2,256,128]{3,2,1,0:T(8,128)S(1)}, f32[2,2,256,128]{3,2,1,0:T(8,128)}, u32[]{:S(2)}, u32[]{:S(2)}) collective-permute-start(f32[2,2,256,128]{3,2,1,0:T(8,128)S(1)} %fusion.61), channel_id=1, source_target_pairs={{0,4},{4,12},{12,8},{8,9},{9,13},{13,5},{5,1},{1,2},{2,6},{6,14},{... | collective-permute-start | bytes 1572872 | tf_op jit(solution)/shard_map/ppermute | solution.py:98
  243.0 12.0 %collective-permute-start.26 = (f32[2,2,256,128]{3,2,0,1:T(8,128)}, f32[2,2,256,128]{3,2,0,1:T(8,128)}, u32[]{:S(2)}, u32[]{:S(2)}) collective-permute-start(f32[2,2,256,128]{3,2,0,1:T(8,128)} %copy.282), channel_id=1, source_target_pairs={{4,0},{12,4},{8,12},{9,8},{13,9},{5,13},{1,5},{2,1},{6,2},{14,6},{... | collective-permute-start | bytes 1572872 | tf_op jit(solution)/shard_map/ppermute | solution.py:98
  256.3 1.6 copy-start.2

commit v2 on v1

--- a/solution.py
+++ b/solution.py
@@ -126,28 +126,284 @@
     return jnp.stack([oy * w - oz * v, oz * u - ox * w, ox * v - oy * u], axis=1)
 
 
-def shards(state, source_mask, deriv_x, deriv_z, filter_x, filter_z):
-    streams, slabs = lax.axis_size("stream"), lax.axis_size("slab")
-    place, order = chain(streams, slabs)
-    fields = state[0]
-    count, width_x, width_y, nz = fields.shape
-    nx = width_x * streams
-    rows = width_y // streams
-    even = lax.axis_index("slab") % 2 == 0
-    back = [streams - 1 - p for p in place]
-
-    parts = fields.reshape(count, width_x, streams, rows, nz).transpose(2, 3, 0, 1, 4)
-    parts = jnp.where(even, jnp.stack([parts[p] for p in place]), jnp.stack([parts[p] for p in back]))
-    parts = lax.all_to_all(parts, "stream", split_axis=0, concat_axis=0, tiled=True)
-    fields = parts.transpose(1, 2, 0, 3, 4).reshape(rows, count, nx, nz)
-
-    blocks = source_mask.astype(jnp.float32)
-    region = jnp.repeat(jnp.repeat(blocks, MBLK, axis=0), MBLK, axis=1).T
-    mine = jnp.asarray(place)[lax.axis_index("stream")]
-    mine = jnp.where(even, mine, streams - 1 - mine)
-    region = lax.dynamic_slice_in_dim(region, mine * rows, rows, 0)[:, None, :, None]
-    deriv_zt, filter_zt = deriv_z.T, filter_z.T
-
+def shift_masked(value, dim, step):
+    size = value.shape[dim]
+    moved = pltpu.roll(value, (-step) % size, dim)
+    index = lax.broadcasted_iota(jnp.int32, value.shape, dim)
+    return jnp.where(index == (size - 1 if step > 0 else 0), 0.0, moved)
+
+
+def inner_slope(value, dim):
+    return 0.5 * (shift_masked(value, dim, 1) - shift_masked(value, dim, -1))
+
+
+def fold(index, side):
+    row = index // side
+    col = index % side
+    return row * side + col + (row % 2) * (side - 1 - 2 * col)
+
+
+def steps_kernel(streams, slabs, pv_ref, uw_ref, region_ref, dx_ref, dzt_ref, fx_ref, fzt_ref, out_ref,
+                 pv, uw, part, source, forcing, dxs, dzs, pv_send, pv_recv, uw_send, uw_recv, src_send, src_recv, credit):
+    rows, _, nx, nz = pv_ref.shape
+    total = streams * slabs
+    side = math.isqrt(streams)
+    side = side if side * side == streams else streams
+    section, stream, slab = lax.axis_index("section"), lax.axis_index("stream"), lax.axis_index("slab")
+
+    def turn(place, which):
+        return place + (which % 2) * (streams - 1 - 2 * place)
+
+    def device_at(spot):
+        which = spot // streams
+        return (section, fold(turn(spot % streams, which), side), which)
+
+    spot = slab * streams + turn(fold(stream, side), slab)
+    has_low, has_high = spot > 0, spot < total - 1
+    low = device_at(jnp.maximum(spot - 1, 0))
+    high = device_at(jnp.minimum(spot + 1, total - 1))
+    partner = (1 - section, stream, slab)
+    is_flow, is_sound = section == 0, section == 1
+
+    def remote(src, dst, send, recv, device):
+        return pltpu.make_async_remote_copy(
+            src_ref=src, dst_ref=dst, send_sem=send, recv_sem=recv,
+            device_id=device, device_id_type=pl.DeviceIdType.MESH,
+        )
+
+    def pv_up(slot):
+        return remote(pv.at[slot, pl.ds(rows, 2)], pv.at[slot, pl.ds(0, 2)], pv_send.at[slot, 0], pv_recv.at[slot, 0], high)
+
+    def pv_down(slot):
+        return remote(pv.at[slot, pl.ds(2, 2)], pv.at[slot, pl.ds(rows + 2, 2)], pv_send.at[slot, 1], pv_recv.at[slot, 1], low)
+
+    def uw_up():
+        return remote(uw.at[rows], uw.at[0], uw_send.at[0], uw_recv.at[0], high)
+
+    def uw_down():
+        return remote(uw.at[1], uw.at[rows + 1], uw_send.at[1], uw_recv.at[1], low)
+
+    def src_copy():
+        return remote(source, forcing, src_send, src_recv, partner)
+
+    def start_both(up, down):
+        @pl.when(has_high)
+        def _():
+            up.start()
+
+        @pl.when(has_low)
+        def _():
+            down.start()
+
+    def wait_both(up, down):
+        @pl.when(has_low)
+        def _():
+            up.wait_recv()
+            down.wait_send()
+
+        @pl.when(has_high)
+        def _():
+            down.wait_recv()
+            up.wait_send()
+
+    def start_uw():
+        @pl.when(is_flow)
+        def _():
+            start_both(uw_up(), uw_down())
+
+    def each_row(body):
+        def step(row, carry):
+            body(row)
+            return carry
+
+        lax.fori_loop(0, rows, step, 0)
+
+    for slot in range(2):
+        for edge in range(2):
+            pv[slot, edge] = jnp.zeros((2, nx, nz), jnp.float32)
+            pv[slot, rows + 2 + edge] = jnp.zeros((2, nx, nz), jnp.float32)
+    uw[0] = jnp.zeros((2, nx, nz), jnp.float32)
+    uw[rows + 1] = jnp.zeros((2, nx, nz), jnp.float32)
+
+    def load(row):
+        pv[0, row + 2] = pv_ref[row]
+        uw[row + 1] = uw_ref[row]
+
+    each_row(load)
+
+    barrier = pltpu.get_barrier_semaphore()
+
+    def greet(device):
+        pl.semaphore_signal(barrier, inc=1, device_id=device, device_id_type=pl.DeviceIdType.MESH)
+
+    greet(partner)
+
+    @pl.when(has_low)
+    def _():
+        greet(low)
+
+    @pl.when(has_high)
+    def _():
+        greet(high)
+
+    pl.semaphore_wait(barrier, 1 + has_low.astype(jnp.int32) + has_high.astype(jnp.int32))
+
+    def put_matrix(mat_x, mat_z):
+        dxs[0], dxs[1] = split_parts(mat_x[...])
+        dzs[0], dzs[1] = split_parts(mat_z[...])
+
+    def operators(slot):
+        def body(row):
+            p, v, u, w = pv[slot, row + 2, 0], pv[slot, row + 2, 1], uw[row + 1, 0], uw[row + 1, 1]
+            sx = dot_parts((dxs[0], dxs[1]), split_parts(jnp.concatenate([p, u, v, w], axis=1)))
+            sz = dot_parts(split_parts(jnp.concatenate([p, w], axis=0)), (dzs[0], dzs[1]))
+            sp, su, sv, sw = (sx[:, i * nz:(i + 1) * nz] for i in range(4))
+            part[row, 0] = p - time_step * (mach_number * sp + su + sz[nx:])
+            part[row, 1] = u - time_step * (mach_number * su + sp)
+            part[row, 2] = v - (time_step * mach_number) * sv
+            part[row, 3] = w - time_step * (mach_number * sw + sz[:nx])
+
+        each_row(body)
+
+    def add_forcing():
+        def body(row):
+            for i in range(3):
+                part[row, i + 1] = part[row, i + 1] + time_step * forcing[row, i]
+
+        each_row(body)
+
+    def keep_uw():
+        def body(row):
+            uw[row + 1, 0] = part[row, 1]
+            uw[row + 1, 1] = part[row, 3]
+
+        each_row(body)
+
+    def update_pv(slot):
+        def body(row):
+            def dy(field):
+                ahead = pv[slot, row + 3, field] - pv[slot, row + 1, field]
+                return (8.0 * ahead - (pv[slot, row + 4, field] - pv[slot, row, field])) / 12.0
+
+            pv[1 - slot, row + 2, 0] = part[row, 0] - time_step * dy(1)
+            pv[1 - slot, row + 2, 1] = part[row, 2] - time_step * dy(0)
+
+        each_row(body)
+
+    def lamb_rows():
+        def body(row):
+            u, v, w = uw[row + 1, 0], pv[0, row + 2, 1], uw[row + 1, 1]
+            ox = 0.5 * (uw[row + 2, 1] - uw[row, 1]) - inner_slope(v, 1)
+            oy = inner_slope(u, 1) - inner_slope(w, 0)
+            oz = inner_slope(v, 0) - 0.5 * (uw[row + 2, 0] - uw[row, 0])
+            mask = -region_ref[row]
+            source[row, 0] = mask * (oy * w - oz * v)
+            source[row, 1] = mask * (oz * u - ox * w)
+            source[row, 2] = mask * (ox * v - oy * u)
+
+        each_row(body)
+
+    put_matrix(dx_ref, dzt_ref)
+    start_uw()
+    start_both(pv_up(0), pv_down(0))
+    pairs = SEGMENTS // 2
+
+    def pair(m, carry):
+        operators(0)
+
+        @pl.when(is_flow)
+        def _():
+            wait_both(uw_up(), uw_down())
+            lamb_rows()
+
+            @pl.when(m > 0)
+            def _():
+                pl.semaphore_wait(credit, 1)
+
+            src_copy().start()
+
+        @pl.when(is_sound)
+        def _():
+            src_copy().wait_recv()
+            add_forcing()
+
+        wait_both(pv_up(0), pv_down(0))
+        update_pv(0)
+        start_both(pv_up(1), pv_down(1))
+        keep_uw()
+        operators(1)
+
+        @pl.when(is_sound)
+        def _():
+            add_forcing()
+
+            @pl.when(m < pairs - 1)
+            def _():
+                pl.semaphore_signal(credit, inc=1, device_id=partner, device_id_type=pl.DeviceIdType.MESH)
+
+        @pl.when(is_flow)
+        def _():
+            src_copy().wait_send()
+
+        keep_uw()
+        wait_both(pv_up(1), pv_down(1))
+
+        @pl.when(m < pairs - 1)
+        def _():
+            start_uw()
+
+        update_pv(1)
+
+        @pl.when(m < pairs - 1)
+        def _():
+            start_both(pv_up(0), pv_down(0))
+
+        return carry
+
+    lax.fori_loop(0, pairs, pair, 0)
+
+    put_matrix(fx_ref, fzt_ref)
+
+    def smooth(row):
+        group = (pv[0, row + 2, 0], uw[row + 1, 0], pv[0, row + 2, 1], uw[row + 1, 1])
+        sx = dot_parts((dxs[0], dxs[1]), split_parts(jnp.concatenate(group, axis=1)))
+        sz = dot_parts(split_parts(jnp.concatenate(group, axis=0)), (dzs[0], dzs[1]))
+        for i in range(4):
+            out_ref[row, i] = group[i] + filter_weight * (sx[:, i * nz:(i + 1) * nz] + sz[i * nx:(i + 1) * nx])
+
+    each_row(smooth)
+
+
+def steps_call(streams, slabs, fields, region, deriv_x, deriv_zt, filter_x, filter_zt):
+    rows, count, nx, nz = fields.shape
+    pv = jnp.stack([fields[:, 0], fields[:, 2]], axis=1)
+    uw = jnp.stack([fields[:, 1], fields[:, 3]], axis=1)
+    f32 = jnp.float32
+    dma = pltpu.SemaphoreType.DMA
+    return pl.pallas_call(
+        functools.partial(steps_kernel, streams, slabs),
+        out_shape=jax.ShapeDtypeStruct(fields.shape, f32),
+        in_specs=[pl.BlockSpec(memory_space=pltpu.VMEM)] * 7,
+        out_specs=pl.BlockSpec(memory_space=pltpu.VMEM),
+        scratch_shapes=[
+            pltpu.VMEM((2, rows + 4, 2, nx, nz), f32),
+            pltpu.VMEM((rows + 2, 2, nx, nz), f32),
+            pltpu.VMEM((rows, 4, nx, nz), f32),
+            pltpu.VMEM((rows, 3, nx, nz), f32),
+            pltpu.VMEM((rows, 3, nx, nz), f32),
+            pltpu.VMEM((2, nx, nx), jnp.bfloat16),
+            pltpu.VMEM((2, nz, nz), jnp.bfloat16),
+            dma((2, 2)), dma((2, 2)), dma((2,)), dma((2,)), dma, dma,
+            pltpu.SemaphoreType.REGULAR,
+        ],
+        compiler_params=pltpu.CompilerParams(
+            collective_id=0, has_side_effects=True, vmem_limit_bytes=48 * 1024 * 1024
+        ),
+    )(pv, uw, jnp.broadcast_to(region, (rows, nx, nz)), deriv_x, deriv_zt, filter_x, filter_zt)
+
+
+def plain_steps(order, fields, region, deriv_x, deriv_zt, filter_x, filter_zt):
+    rows = fields.shape[0]
     forcing = None
     for segment in range(SEGMENTS):
         pv = jnp.stack([fields[:, 0], fields[:, 2]], axis=1)
@@ -169,7 +425,36 @@
             ],
             axis=1,
         )
-    fields = row_call(filter_kernel, fields, filter_x, filter_zt)
+    return row_call(filter_kernel, fields, filter_x, filter_zt)
+
+
+def shards(state, source_mask, deriv_x, deriv_z, filter_x, filter_z):
+    streams, slabs = lax.axis_size("stream"), lax.axis_size("slab")
+    place, order = chain(streams, slabs)
+    fields = state[0]
+    count, width_x, width_y, nz = fields.shape
+    nx = width_x * streams
+    rows = width_y // streams
+    even = lax.axis_index("slab") % 2 == 0
+    back = [streams - 1 - p for p in place]
+
+    parts = fields.reshape(count, width_x, streams, rows, nz).transpose(2, 3, 0, 1, 4)
+    parts = jnp.where(even, jnp.stack([parts[p] for p in place]), jnp.stack([parts[p] for p in back]))
+    parts = lax.all_to_all(parts, "stream", split_axis=0, concat_axis=0, tiled=True)
+    fields = parts.transpose(1, 2, 0, 3, 4).reshape(rows, count, nx, nz)
+
+    blocks = source_mask.astype(jnp.float32)
+    region = jnp.repeat(jnp.repeat(blocks, MBLK, axis=0), MBLK, axis=1).T
+    mine = jnp.asarray(place)[lax.axis_index("stream")]
+    mine = jnp.where(even, mine, streams - 1 - mine)
+    region = lax.dynamic_slice_in_dim(region, mine * rows, rows, 0)[:, None, :, None]
+    deriv_zt, filter_zt = deriv_z.T, filter_z.T
+
+    mats = (deriv_x, deriv_zt, filter_x, filter_zt)
+    if rows >= 2:
+        fields = steps_call(streams, slabs, fields, region[:, 0], *mats)
+    else:
+        fields = plain_steps(order, fields, region, *mats)
 
     parts = fields.reshape(rows, count, streams, width_x, nz).transpose(2, 0, 1, 3, 4)
     parts = lax.all_to_all(parts, "stream", split_axis=0, concat_axis=0, tiled=True)

time: 293 us -> 177 us (0.60)
  starting transfers between devices: 78.3 us -> 3.85 us
  Pallas kernels: 43.1 us -> 110 us
  other arithmetic: 42.3 us -> 2.25 us
  local copies, waits for them, and re-layouts: 35.4 us -> 7.17 us
  blocking collectives: 49 us -> 26.7 us
  waiting for transfers between devices: 42.3 us -> 24.6 us
    ppermute x28 -> x0, starting transfers between devices: 78.3 us -> none  [the longest x24 70.4 us: shift(): return lax.ppermute(part, axes, pairs)]
    pallas_call x9 -> x1, Pallas kernels: 43.1 us -> 110 us  [steps_call(): pl.pallas_call(functools.partial(steps_kernel, streams, slabs), out_shape...]
    ppermute x28 -> x0, waiting for transfers between devices: 42.3 us -> none  [the longest x24 42.3 us: shift(): return lax.ppermute(part, axes, pairs)]
    all_to_all x0 -> x1, waiting for transfers between devices: none -> 24.6 us  [shards(): lax.all_to_all(parts, 'stream', split_axis=0, concat_axis=0, tiled=True)]
    all_to_all x2 -> x1, blocking collectives: 49 us -> 26.7 us  [shards(): lax.all_to_all(parts, 'stream', split_axis=0, concat_axis=0, tiled=True)]
    unnamed x41 -> x13, local copies, waits for them, and re-layouts: 17.2 us -> 3.17 us
    another operation x25 -> x1, other arithmetic: 14.1 us -> 0.19 us  [steps_call(): pv = jnp.stack([fields[:, 0], fields[:, 2]], axis=1)]
    add x11 -> x0, other arithmetic: 10 us -> none  [the longest x8 7.03 us: shards(): part[:, 1] + time_step * forcing[:, 0]]
  transfers between devices with their start and end apart: 28 -> 1, of which waited for: 17 -> 1; matrix products, arithmetic and copies ran while one was open for 10% -> 0% of each run, Pallas kernels for 13% -> 0%
where the time goes in v2:
time: 177 us; the launch traced here: 175 us
  Pallas kernels  110 us (62%)
  blocking collectives  26.7 us (15%)
  waiting for transfers between devices  24.6 us (14%)
  local copies, waits for them, and re-layouts  7.17 us (4%)
  starting transfers between devices  3.85 us (2%)
  other arithmetic  2.25 us (1%)
    pallas_call x1, Pallas kernels, steps_call(): pl.pallas_call(functools.partial(steps_kernel, streams, slabs), out_shape...  110 us
    all_to_all x1, blocking collectives, shards(): lax.all_to_all(parts, 'stream', split_axis=0, concat_axis=0, tiled=True)  26.7 us
    all_to_all x1, waiting for transfers between devices, shards(): lax.all_to_all(parts, 'stream', split_axis=0, concat_axis=0, tiled=True)  24.6 us
    all_to_all x1, starting transfers between devices, shards(): lax.all_to_all(parts, 'stream', split_axis=0, concat_axis=0, tiled=True)  3.85 us
  transfers between devices with their start and end apart: 1, of which 1 were waited for; matrix products, arithmetic and copies ran while one was open for 0% of the time, Pallas kernels for 0%

profile of v2, /device:TPU:16, one launch (start us, length us, event | category | flops | bytes accessed | tf_op | source)
XLA Modules:
  0.0 175.2 jit_solution(14650226642580252491)
XLA Ops:
  0.0 2.3 %copy.11 = f32[1,4,64,16,128]{4,2,1,3,0:T(8,128)S(1)} copy(f32[1,4,64,16,128]{4,3,2,1,0:T(8,128)} %param.6) | data formatting | bytes 4194304 | tf_op args[0]
  2.3 0.1 slice.63
  2.4 0.1 fusion.3
  2.5 1.5 maximum_select_fusion
  4.0 0.0 copy-start.4
  4.0 0.0 copy-start.2
  4.0 0.0 copy-start.3
  4.0 3.8 %all-to-all-start = ((f32[4,4,4,64,128]{4,3,2,1,0:T(8,128)}), f32[4,4,4,64,128]{4,3,2,1,0:T(8,128)S(1)}, u32[]{:S(2)}, u32[]{:S(2)}) async-start(f32[4,4,4,64,128]{4,3,2,1,0:T(8,128)} %maximum_select_fusion), calls=%async_computation | async-start | bytes 4194304 | tf_op jit(solution)/shard_map/all_to_all | solution.py:443
  7.9 0.0 copy-done.4
  7.9 0.1 broadcast_in_dim.11
  7.9 0.1 broadcast_in_dim.12
  8.0 0.0 copy-done.2
  8.0 0.1 copy.13
  8.1 0.0 copy-done.3
  8.1 0.1 copy.14
  8.2 24.6 %all-to-all-done = f32[4,4,4,64,128]{4,3,2,1,0:T(8,128)S(1)} async-done(((f32[4,4,4,64,128]{4,3,2,1,0:T(8,128)}), f32[4,4,4,64,128]{4,3,2,1,0:T(8,128)S(1)}, u32[]{:S(2)}, u32[]{:S(2)}) %all-to-all-start) | async-done | bytes 2097184 | tf_op jit(solution)/shard_map/all_to_all | solution.py:443
  32.9 0.2 copy.12
  33.1 0.1 fusion.2
  33.3 0.0 copy-start
  33.3 0.0 copy-start.1
  33.3 0.2 pad_maximum_fusion
  33.5 0.1 broadcast_in_dim.13.region_ref
  33.6 0.6 copy-done
  34.2 0.1 copy-done.1
  34.3 110.4 %shard_map.69 = f32[4,4,256,128]{3,2,1,0:T(8,128)S(1)} custom-call(f32[4,2,256,128]{3,2,1,0:T(8,128)S(1)} %get-tuple-element.17.pv_ref, f32[4,2,256,128]{3,2,1,0:T(8,128)S(1)} %get-tuple-element.18.uw_ref, f32[4,256,128]{2,1,0:T(8,128)S(1)} %broadcast_in_dim.13.region_ref, f32[256,256]{1,0:T(8,128)S(1)} %copy-done, f32[128,128]{1,0:T(8,128)S(1)} %bitcast.17, ...), custom_call_target="tpu_custom_call" | custom-call | tf_op jit(solution)/shard_map/pallas_call | solution.py:383
  144.7 0.1 copy.18
  144.9 26.7 %all_to_all.10 = f32[4,4,4,64,128]{4,3,2,1,0:T(8,128)S(1)} all-to-all(f32[4,4,4,64,128]{4,3,2,1,0:T(8,128)S(1)} %bitcast.24), channel_id=1, replica_groups=mesh['section'=2,'stream'=4,'slab'=4] {'stream'}, dimensions={0} | all-to-all | bytes 4194304 | tf_op jit(solution)/shard_map/all_to_all | solution.py:460
  171.5 0.2 fusion.1
  171.8 0.2 fusion
  172.0 0.6 maximum_select_fusion.1
  172.6 2.5 %copy.16 = f32[1,4,64,16,128]{4,3,2,1,0:T(8,128)} copy(f32[1,4,64,16,128]{4,2,1,3,0:T(8,128)S(1)} %bitcast.19) | data formatting | bytes 4194304 | tf_op jit(solution)/shard_map/reshape | solution.py:464
  (1 shorter events, 0.0 us)
Async XLA Ops:
  4.0 3.9 %copy-start.4 = (s32[16,1]{0,1:T(1,128)S(1)}, s32[16,1]{0,1:T(1,128)}, u32[]{:S(2)}) copy-start(s32[16,1]{0,1:T(1,128)} %param.7) | copy-start | bytes 196
  4.0 4.0 %copy-start.2 = (f32[128,128]{1,0:T(8,128)S(1)}, f32[128,128]{1,0:T(8,128)}, u32[]{:S(2)}) copy-start(f32[128,128]{1,0:T(8,128)} %param.9) | copy-start | bytes 196612
  4.0 4.1 %copy-start.3 = (f32[128,128]{1,0:T(8,128)S(1)}, f32[128,128]{1,0:T(8,128)}, u32[]{:S(2)}) copy-start(f32[128,128]{1,0:T(8,128)} %param.11) | copy-start | bytes 196612
  4.0 28.9 %all-to-all-start = ((f32[4,4,4,64,128]{4,3,2,1,0:T(8,128)}), f32[4,4,4,64,128]{4,3,2,1,0:T(8,128)S(1)}, u32[]{:S(2)}, u32[]{:S(2)}) async-start(f32[4,4,4,64,128]{4,3,2,1,0:T(8,128)} %maximum_select_fusion), calls=%async_computation | async-start | bytes 4194304 | tf_op jit(solution)/shard_map/all_to_all | solution.py:443
  33.3 1.0 copy-start
  33.3 1.0 copy-start.1

commit v3 on v2

--- a/solution.py
+++ b/solution.py
@@ -144,7 +144,7 @@
 
 
 def steps_kernel(streams, slabs, pv_ref, uw_ref, region_ref, dx_ref, dzt_ref, fx_ref, fzt_ref, out_ref,
-                 pv, uw, part, source, forcing, dxs, dzs, pv_send, pv_recv, uw_send, uw_recv, src_send, src_recv, credit):
+                 pv, uw, edge, part, source, forcing, dxs, dzs, pv_send, pv_recv, uw_send, uw_recv, src_send, src_recv, credit):
     rows, _, nx, nz = pv_ref.shape
     total = streams * slabs
     side = math.isqrt(streams)
@@ -219,9 +219,9 @@
         lax.fori_loop(0, rows, step, 0)
 
     for slot in range(2):
-        for edge in range(2):
-            pv[slot, edge] = jnp.zeros((2, nx, nz), jnp.float32)
-            pv[slot, rows + 2 + edge] = jnp.zeros((2, nx, nz), jnp.float32)
+        for line in range(2):
+            pv[slot, line] = jnp.zeros((2, nx, nz), jnp.float32)
+            pv[slot, rows + 2 + line] = jnp.zeros((2, nx, nz), jnp.float32)
     uw[0] = jnp.zeros((2, nx, nz), jnp.float32)
     uw[rows + 1] = jnp.zeros((2, nx, nz), jnp.float32)
 
@@ -303,17 +303,37 @@
 
         each_row(body)
 
+    def keep_edge(slot):
+        edge[0] = pv[slot, 1, 0]
+        edge[1] = pv[slot, rows + 2, 0]
+
+    def advance_edges():
+        def body(which, carry):
+            row = which * (rows + 1)
+            p, u, w = edge[which], uw[row, 0], uw[row, 1]
+            sx = dot_parts((dxs[0], dxs[1]), split_parts(jnp.concatenate([p, u, w], axis=1)))
+            sz = dot_parts(split_parts(p), (dzs[0], dzs[1]))
+            sp, su, sw = (sx[:, i * nz:(i + 1) * nz] for i in range(3))
+            uw[row, 0] = u - time_step * (mach_number * su + sp)
+            uw[row, 1] = w - time_step * (mach_number * sw + sz)
+            return carry
+
+        @pl.when(is_flow)
+        def _():
+            lax.fori_loop(0, 2, body, 0)
+
     put_matrix(dx_ref, dzt_ref)
     start_uw()
     start_both(pv_up(0), pv_down(0))
     pairs = SEGMENTS // 2
 
     def pair(m, carry):
-        operators(0)
-
         @pl.when(is_flow)
         def _():
-            wait_both(uw_up(), uw_down())
+            @pl.when(m == 0)
+            def _():
+                wait_both(uw_up(), uw_down())
+
             lamb_rows()
 
             @pl.when(m > 0)
@@ -322,6 +342,8 @@
 
             src_copy().start()
 
+        operators(0)
+
         @pl.when(is_sound)
         def _():
             src_copy().wait_recv()
@@ -329,6 +351,7 @@
 
         wait_both(pv_up(0), pv_down(0))
         update_pv(0)
+        keep_edge(0)
         start_both(pv_up(1), pv_down(1))
         keep_uw()
         operators(1)
@@ -346,17 +369,15 @@
             src_copy().wait_send()
 
         keep_uw()
+        advance_edges()
         wait_both(pv_up(1), pv_down(1))
+        update_pv(1)
 
         @pl.when(m < pairs - 1)
         def _():
-            start_uw()
-
-        update_pv(1)
-
-        @pl.when(m < pairs - 1)
-        def _():
+            keep_edge(1)
             start_both(pv_up(0), pv_down(0))
+            advance_edges()
 
         return carry
 
@@ -388,6 +409,7 @@
         scratch_shapes=[
             pltpu.VMEM((2, rows + 4, 2, nx, nz), f32),
             pltpu.VMEM((rows + 2, 2, nx, nz), f32),
+            pltpu.VMEM((2, nx, nz), f32),
             pltpu.VMEM((rows, 4, nx, nz), f32),
             pltpu.VMEM((rows, 3, nx, nz), f32),
             pltpu.VMEM((rows, 3, nx, nz), f32),

time: 177 us -> 164 us (0.927)
  Pallas kernels: 110 us -> 98.6 us
    pallas_call x1, Pallas kernels: 110 us -> 98.6 us  [steps_call(): pl.pallas_call(functools.partial(steps_kernel, streams, slabs), out_shape...]
where the time goes in v3:
time: 164 us; the launch traced here: 162 us
  Pallas kernels  98.6 us (60%)
  blocking collectives  25.5 us (16%)
  waiting for transfers between devices  24.6 us (15%)
  local copies, waits for them, and re-layouts  7.17 us (4%)
  starting transfers between devices  3.85 us (2%)
  other arithmetic  2.25 us (1%)
    pallas_call x1, Pallas kernels, steps_call(): pl.pallas_call(functools.partial(steps_kernel, streams, slabs), out_shape...  98.6 us
    all_to_all x1, blocking collectives, shards(): lax.all_to_all(parts, 'stream', split_axis=0, concat_axis=0, tiled=True)  25.5 us
    all_to_all x1, waiting for transfers between devices, shards(): lax.all_to_all(parts, 'stream', split_axis=0, concat_axis=0, tiled=True)  24.6 us
    all_to_all x1, starting transfers between devices, shards(): lax.all_to_all(parts, 'stream', split_axis=0, concat_axis=0, tiled=True)  3.85 us
  transfers between devices with their start and end apart: 1, of which 1 were waited for; matrix products, arithmetic and copies ran while one was open for 0% of the time, Pallas kernels for 0%

profile of v3, /device:TPU:16, one launch (start us, length us, event | category | flops | bytes accessed | tf_op | source)
XLA Modules:
  0.0 162.2 jit_solution(656104234950728154)
XLA Ops:
  0.0 2.3 %copy.11 = f32[1,4,64,16,128]{4,2,1,3,0:T(8,128)S(1)} copy(f32[1,4,64,16,128]{4,3,2,1,0:T(8,128)} %param.6) | data formatting | bytes 4194304 | tf_op args[0]
  2.3 0.1 slice.63
  2.4 0.1 fusion.3
  2.5 1.5 maximum_select_fusion
  4.0 0.0 copy-start.4
  4.0 0.0 copy-start.2
  4.0 0.0 copy-start.3
  4.0 3.8 %all-to-all-start = ((f32[4,4,4,64,128]{4,3,2,1,0:T(8,128)}), f32[4,4,4,64,128]{4,3,2,1,0:T(8,128)S(1)}, u32[]{:S(2)}, u32[]{:S(2)}) async-start(f32[4,4,4,64,128]{4,3,2,1,0:T(8,128)} %maximum_select_fusion), calls=%async_computation | async-start | bytes 4194304 | tf_op jit(solution)/shard_map/all_to_all | solution.py:465
  7.9 0.0 copy-done.4
  7.9 0.1 broadcast_in_dim.11
  7.9 0.1 broadcast_in_dim.12
  8.0 0.0 copy-done.2
  8.0 0.1 copy.13
  8.1 0.0 copy-done.3
  8.1 0.1 copy.14
  8.2 24.6 %all-to-all-done = f32[4,4,4,64,128]{4,3,2,1,0:T(8,128)S(1)} async-done(((f32[4,4,4,64,128]{4,3,2,1,0:T(8,128)}), f32[4,4,4,64,128]{4,3,2,1,0:T(8,128)S(1)}, u32[]{:S(2)}, u32[]{:S(2)}) %all-to-all-start) | async-done | bytes 2097184 | tf_op jit(solution)/shard_map/all_to_all | solution.py:465
  32.9 0.2 copy.12
  33.1 0.1 fusion.2
  33.3 0.0 copy-start
  33.3 0.0 copy-start.1
  33.3 0.2 pad_maximum_fusion
  33.5 0.1 broadcast_in_dim.13.region_ref
  33.6 0.6 copy-done
  34.2 0.1 copy-done.1
  34.3 98.6 %shard_map.69 = f32[4,4,256,128]{3,2,1,0:T(8,128)S(1)} custom-call(f32[4,2,256,128]{3,2,1,0:T(8,128)S(1)} %get-tuple-element.17.pv_ref, f32[4,2,256,128]{3,2,1,0:T(8,128)S(1)} %get-tuple-element.18.uw_ref, f32[4,256,128]{2,1,0:T(8,128)S(1)} %broadcast_in_dim.13.region_ref, f32[256,256]{1,0:T(8,128)S(1)} %copy-done, f32[128,128]{1,0:T(8,128)S(1)} %bitcast.17, ...), custom_call_target="tpu_custom_call" | custom-call | tf_op jit(solution)/shard_map/pallas_call | solution.py:404
  133.0 0.1 copy.18
  133.1 25.5 %all_to_all.10 = f32[4,4,4,64,128]{4,3,2,1,0:T(8,128)S(1)} all-to-all(f32[4,4,4,64,128]{4,3,2,1,0:T(8,128)S(1)} %bitcast.24), channel_id=1, replica_groups=mesh['section'=2,'stream'=4,'slab'=4] {'stream'}, dimensions={0} | all-to-all | bytes 4194304 | tf_op jit(solution)/shard_map/all_to_all | solution.py:482
  158.6 0.2 fusion.1
  158.9 0.2 fusion
  159.1 0.6 maximum_select_fusion.1
  159.7 2.5 %copy.16 = f32[1,4,64,16,128]{4,3,2,1,0:T(8,128)} copy(f32[1,4,64,16,128]{4,2,1,3,0:T(8,128)S(1)} %bitcast.19) | data formatting | bytes 4194304 | tf_op jit(solution)/shard_map/reshape | solution.py:486
  (1 shorter events, 0.0 us)
Async XLA Ops:
  4.0 3.9 %copy-start.4 = (s32[16,1]{0,1:T(1,128)S(1)}, s32[16,1]{0,1:T(1,128)}, u32[]{:S(2)}) copy-start(s32[16,1]{0,1:T(1,128)} %param.7) | copy-start | bytes 196
  4.0 4.0 %copy-start.2 = (f32[128,128]{1,0:T(8,128)S(1)}, f32[128,128]{1,0:T(8,128)}, u32[]{:S(2)}) copy-start(f32[128,128]{1,0:T(8,128)} %param.9) | copy-start | bytes 196612
  4.0 4.1 %copy-start.3 = (f32[128,128]{1,0:T(8,128)S(1)}, f32[128,128]{1,0:T(8,128)}, u32[]{:S(2)}) copy-start(f32[128,128]{1,0:T(8,128)} %param.11) | copy-start | bytes 196612
  4.0 28.9 %all-to-all-start = ((f32[4,4,4,64,128]{4,3,2,1,0:T(8,128)}), f32[4,4,4,64,128]{4,3,2,1,0:T(8,128)S(1)}, u32[]{:S(2)}, u32[]{:S(2)}) async-start(f32[4,4,4,64,128]{4,3,2,1,0:T(8,128)} %maximum_select_fusion), calls=%async_computation | async-start | bytes 4194304 | tf_op jit(solution)/shard_map/all_to_all | solution.py:465
  33.3 1.0 copy-start
  33.3 1.0 copy-start.1

commit v4 on v3

--- a/solution.py
+++ b/solution.py
@@ -144,7 +144,7 @@
 
 
 def steps_kernel(streams, slabs, pv_ref, uw_ref, region_ref, dx_ref, dzt_ref, fx_ref, fzt_ref, out_ref,
-                 pv, uw, edge, part, source, forcing, dxs, dzs, pv_send, pv_recv, uw_send, uw_recv, src_send, src_recv, credit):
+                 pv, uw, edge, part, source, forcing, dxs, dzs, pv_send, pv_recv, uw_send, uw_recv, src_send, src_recv, row_send, row_recv, credit):
     rows, _, nx, nz = pv_ref.shape
     total = streams * slabs
     side = math.isqrt(streams)
@@ -237,16 +237,20 @@
         pl.semaphore_signal(barrier, inc=1, device_id=device, device_id_type=pl.DeviceIdType.MESH)
 
     greet(partner)
-
-    @pl.when(has_low)
+    for t in range(1, streams):
+        greet((section, (stream + t) % streams, slab))
+    low_apart = has_low & (spot % streams == 0)
+    high_apart = has_high & (spot % streams == streams - 1)
+
+    @pl.when(low_apart)
     def _():
         greet(low)
 
-    @pl.when(has_high)
+    @pl.when(high_apart)
     def _():
         greet(high)
 
-    pl.semaphore_wait(barrier, 1 + has_low.astype(jnp.int32) + has_high.astype(jnp.int32))
+    pl.semaphore_wait(barrier, streams + low_apart.astype(jnp.int32) + high_apart.astype(jnp.int32))
 
     def put_matrix(mat_x, mat_z):
         dxs[0], dxs[1] = split_parts(mat_x[...])
@@ -390,9 +394,35 @@
         sx = dot_parts((dxs[0], dxs[1]), split_parts(jnp.concatenate(group, axis=1)))
         sz = dot_parts(split_parts(jnp.concatenate(group, axis=0)), (dzs[0], dzs[1]))
         for i in range(4):
-            out_ref[row, i] = group[i] + filter_weight * (sx[:, i * nz:(i + 1) * nz] + sz[i * nx:(i + 1) * nx])
+            part[row, i] = group[i] + filter_weight * (sx[:, i * nz:(i + 1) * nz] + sz[i * nx:(i + 1) * nx])
+        for t in range(1, streams):
+            row_copy(t, row).start()
+        own = pl.ds(pl.multiple_of(stream * width, width), width)
+        out_ref[chunk_of(stream), row] = part[row, :, own]
+
+    width = nx // streams
+
+    def chunk_of(which):
+        return turn(fold(which, side), slab)
+
+    def row_copy(t, row):
+        peer = (stream + t) % streams
+        cells = pl.ds(pl.multiple_of(peer * width, width), width)
+        return remote(
+            part.at[row, :, cells], out_ref.at[chunk_of(stream), row],
+            row_send.at[t - 1, row], row_recv.at[t - 1, row], (section, peer, slab),
+        )
 
     each_row(smooth)
+
+    def finish(row):
+        for t in range(1, streams):
+            sender = (stream + streams - t) % streams
+            landed = out_ref.at[chunk_of(sender), row]
+            row_copy(t, row).wait_send()
+            remote(landed, landed, row_send.at[t - 1, row], row_recv.at[t - 1, row], (section, sender, slab)).wait_recv()
+
+    each_row(finish)
 
 
 def steps_call(streams, slabs, fields, region, deriv_x, deriv_zt, filter_x, filter_zt):
@@ -403,7 +433,7 @@
     dma = pltpu.SemaphoreType.DMA
     return pl.pallas_call(
         functools.partial(steps_kernel, streams, slabs),
-        out_shape=jax.ShapeDtypeStruct(fields.shape, f32),
+        out_shape=jax.ShapeDtypeStruct((streams, rows, count, nx // streams, nz), f32),
         in_specs=[pl.BlockSpec(memory_space=pltpu.VMEM)] * 7,
         out_specs=pl.BlockSpec(memory_space=pltpu.VMEM),
         scratch_shapes=[
@@ -416,6 +446,7 @@
             pltpu.VMEM((2, nx, nx), jnp.bfloat16),
             pltpu.VMEM((2, nz, nz), jnp.bfloat16),
             dma((2, 2)), dma((2, 2)), dma((2,)), dma((2,)), dma, dma,
+            dma((streams - 1, rows)), dma((streams - 1, rows)),
             pltpu.SemaphoreType.REGULAR,
         ],
         compiler_params=pltpu.CompilerParams(
@@ -474,9 +505,9 @@
 
     mats = (deriv_x, deriv_zt, filter_x, filter_zt)
     if rows >= 2:
-        fields = steps_call(streams, slabs, fields, region[:, 0], *mats)
-    else:
-        fields = plain_steps(order, fields, region, *mats)
+        parts = steps_call(streams, slabs, fields, region[:, 0], *mats)
+        return parts.transpose(2, 3, 0, 1, 4).reshape(1, count, width_x, width_y, nz)
+    fields = plain_steps(order, fields, region, *mats)
 
     parts = fields.reshape(rows, count, streams, width_x, nz).transpose(2, 0, 1, 3, 4)
     parts = lax.all_to_all(parts, "stream", split_axis=0, concat_axis=0, tiled=True)

time: 164 us -> 157 us (0.957)
  blocking collectives: 25.5 us -> 0 us
  Pallas kernels: 98.6 us -> 119 us
    all_to_all x1 -> x0, blocking collectives: 25.5 us -> none  [shards(): lax.all_to_all(parts, 'stream', split_axis=0, concat_axis=0, tiled=True)]
    pallas_call x1, Pallas kernels: 98.6 us -> 119 us  [steps_call(): pl.pallas_call(functools.partial(steps_kernel, streams, slabs), out_shape...]
where the time goes in v4:
time: 157 us; the launch traced here: 156 us
  Pallas kernels  119 us (76%)
  waiting for transfers between devices  24.6 us (16%)
  local copies, waits for them, and re-layouts  6.55 us (4%)
  starting transfers between devices  3.85 us (2%)
  other arithmetic  1.68 us (1%)
    pallas_call x1, Pallas kernels, steps_call(): pl.pallas_call(functools.partial(steps_kernel, streams, slabs), out_shape...  119 us
    all_to_all x1, waiting for transfers between devices, shards(): lax.all_to_all(parts, 'stream', split_axis=0, concat_axis=0, tiled=True)  24.6 us
    all_to_all x1, starting transfers between devices, shards(): lax.all_to_all(parts, 'stream', split_axis=0, concat_axis=0, tiled=True)  3.85 us
    unnamed x13, local copies, waits for them, and re-layouts  3.17 us
  transfers between devices with their start and end apart: 1, of which 1 were waited for; matrix products, arithmetic and copies ran while one was open for 0% of the time, Pallas kernels for 0%

profile of v4, /device:TPU:16, one launch (start us, length us, event | category | flops | bytes accessed | tf_op | source)
XLA Modules:
  0.0 155.6 jit_solution(6735326898283501757)
XLA Ops:
  0.0 2.3 %copy.11 = f32[1,4,64,16,128]{4,2,1,3,0:T(8,128)S(1)} copy(f32[1,4,64,16,128]{4,3,2,1,0:T(8,128)} %param.6) | data formatting | bytes 4194304 | tf_op args[0]
  2.3 0.1 fusion.1
  2.4 0.1 slice.35
  2.5 1.5 maximum_select_fusion
  4.0 0.0 copy-start.4
  4.0 0.0 copy-start.2
  4.0 0.0 copy-start.3
  4.0 3.8 %all-to-all-start = ((f32[4,4,4,64,128]{4,3,2,1,0:T(8,128)}), f32[4,4,4,64,128]{4,3,2,1,0:T(8,128)S(1)}, u32[]{:S(2)}, u32[]{:S(2)}) async-start(f32[4,4,4,64,128]{4,3,2,1,0:T(8,128)} %maximum_select_fusion), calls=%async_computation | async-start | bytes 4194304 | tf_op jit(solution)/shard_map/all_to_all | solution.py:496
  7.9 0.0 copy-done.4
  7.9 0.1 broadcast_in_dim.11
  7.9 0.1 broadcast_in_dim.12
  8.0 0.0 copy-done.2
  8.0 0.1 copy.13
  8.1 0.0 copy-done.3
  8.1 0.1 copy.14
  8.2 24.6 %all-to-all-done = f32[4,4,4,64,128]{4,3,2,1,0:T(8,128)S(1)} async-done(((f32[4,4,4,64,128]{4,3,2,1,0:T(8,128)}), f32[4,4,4,64,128]{4,3,2,1,0:T(8,128)S(1)}, u32[]{:S(2)}, u32[]{:S(2)}) %all-to-all-start) | async-done | bytes 2097184 | tf_op jit(solution)/shard_map/all_to_all | solution.py:496
  32.9 0.2 copy.12
  33.1 0.1 fusion
  33.3 0.0 copy-start
  33.3 0.0 copy-start.1
  33.3 0.2 pad_maximum_fusion
  33.5 0.1 broadcast_in_dim.13.region_ref
  33.6 0.6 copy-done
  34.2 0.1 copy-done.1
  34.3 118.8 %shard_map.69 = f32[4,4,4,64,128]{4,3,2,1,0:T(8,128)S(1)} custom-call(f32[4,2,256,128]{3,2,1,0:T(8,128)S(1)} %get-tuple-element.11.pv_ref, f32[4,2,256,128]{3,2,1,0:T(8,128)S(1)} %get-tuple-element.12.uw_ref, f32[4,256,128]{2,1,0:T(8,128)S(1)} %broadcast_in_dim.13.region_ref, f32[256,256]{1,0:T(8,128)S(1)} %copy-done, f32[128,128]{1,0:T(8,128)S(1)} %bitcast.13, ...), custom_call_target="tpu_custom_call" | custom-call | tf_op jit(solution)/shard_map/pallas_call | solution.py:434
  153.1 2.5 %copy.15 = f32[1,4,64,16,128]{4,3,2,1,0:T(8,128)} copy(f32[1,4,64,16,128]{4,2,1,3,0:T(8,128)S(1)} %bitcast.12) | data formatting | bytes 4194304 | tf_op jit(solution)/shard_map/reshape | solution.py:509
  (1 shorter events, 0.0 us)
Async XLA Ops:
  4.0 3.9 %copy-start.4 = (s32[16,1]{0,1:T(1,128)S(1)}, s32[16,1]{0,1:T(1,128)}, u32[]{:S(2)}) copy-start(s32[16,1]{0,1:T(1,128)} %param.7) | copy-start | bytes 196
  4.0 4.0 %copy-start.2 = (f32[128,128]{1,0:T(8,128)S(1)}, f32[128,128]{1,0:T(8,128)}, u32[]{:S(2)}) copy-start(f32[128,128]{1,0:T(8,128)} %param.9) | copy-start | bytes 196612
  4.0 4.1 %copy-start.3 = (f32[128,128]{1,0:T(8,128)S(1)}, f32[128,128]{1,0:T(8,128)}, u32[]{:S(2)}) copy-start(f32[128,128]{1,0:T(8,128)} %param.11) | copy-start | bytes 196612
  4.0 28.9 %all-to-all-start = ((f32[4,4,4,64,128]{4,3,2,1,0:T(8,128)}), f32[4,4,4,64,128]{4,3,2,1,0:T(8,128)S(1)}, u32[]{:S(2)}, u32[]{:S(2)}) async-start(f32[4,4,4,64,128]{4,3,2,1,0:T(8,128)} %maximum_select_fusion), calls=%async_computation | async-start | bytes 4194304 | tf_op jit(solution)/shard_map/all_to_all | solution.py:496
  33.3 1.0 copy-start
  33.3 1.0 copy-start.1

commit v5 on v4

--- a/solution.py
+++ b/solution.py
@@ -143,9 +143,10 @@
     return row * side + col + (row % 2) * (side - 1 - 2 * col)
 
 
-def steps_kernel(streams, slabs, pv_ref, uw_ref, region_ref, dx_ref, dzt_ref, fx_ref, fzt_ref, out_ref,
-                 pv, uw, edge, part, source, forcing, dxs, dzs, pv_send, pv_recv, uw_send, uw_recv, src_send, src_recv, row_send, row_recv, credit):
-    rows, _, nx, nz = pv_ref.shape
+def steps_kernel(streams, slabs, cells_ref, region_ref, dx_ref, dzt_ref, fx_ref, fzt_ref, out_ref,
+                 pv, uw, edge, part, source, forcing, dxs, dzs, pv_send, pv_recv, uw_send, uw_recv, src_send, src_recv, row_send, row_recv, in_send, in_recv, credit):
+    _, rows, _, width, nz = cells_ref.shape
+    nx = width * streams
     total = streams * slabs
     side = math.isqrt(streams)
     side = side if side * side == streams else streams
@@ -225,12 +226,6 @@
     uw[0] = jnp.zeros((2, nx, nz), jnp.float32)
     uw[rows + 1] = jnp.zeros((2, nx, nz), jnp.float32)
 
-    def load(row):
-        pv[0, row + 2] = pv_ref[row]
-        uw[row + 1] = uw_ref[row]
-
-    each_row(load)
-
     barrier = pltpu.get_barrier_semaphore()
 
     def greet(device):
@@ -251,6 +246,36 @@
         greet(high)
 
     pl.semaphore_wait(barrier, streams + low_apart.astype(jnp.int32) + high_apart.astype(jnp.int32))
+
+    def chunk_of(which):
+        return turn(fold(which, side), slab)
+
+    def axial(which):
+        return pl.ds(pl.multiple_of(which * width, width), width)
+
+    def in_copy(t):
+        peer = (stream + t) % streams
+        return remote(
+            cells_ref.at[chunk_of(peer)], part.at[:, :, axial(stream)],
+            in_send.at[t - 1], in_recv.at[t - 1], (section, peer, slab),
+        )
+
+    for t in range(1, streams):
+        in_copy(t).start()
+    part[:, :, axial(stream)] = cells_ref[chunk_of(stream)]
+    for t in range(1, streams):
+        sender = (stream + streams - t) % streams
+        landed = part.at[:, :, axial(sender)]
+        in_copy(t).wait_send()
+        remote(landed, landed, in_send.at[t - 1], in_recv.at[t - 1], (section, sender, slab)).wait_recv()
+
+    def load(row):
+        pv[0, row + 2, 0] = part[row, 0]
+        pv[0, row + 2, 1] = part[row, 2]
+        uw[row + 1, 0] = part[row, 1]
+        uw[row + 1, 1] = part[row, 3]
+
+    each_row(load)
 
     def put_matrix(mat_x, mat_z):
         dxs[0], dxs[1] = split_parts(mat_x[...])
@@ -400,11 +425,6 @@
         own = pl.ds(pl.multiple_of(stream * width, width), width)
         out_ref[chunk_of(stream), row] = part[row, :, own]
 
-    width = nx // streams
-
-    def chunk_of(which):
-        return turn(fold(which, side), slab)
-
     def row_copy(t, row):
         peer = (stream + t) % streams
         cells = pl.ds(pl.multiple_of(peer * width, width), width)
@@ -425,16 +445,15 @@
     each_row(finish)
 
 
-def steps_call(streams, slabs, fields, region, deriv_x, deriv_zt, filter_x, filter_zt):
-    rows, count, nx, nz = fields.shape
-    pv = jnp.stack([fields[:, 0], fields[:, 2]], axis=1)
-    uw = jnp.stack([fields[:, 1], fields[:, 3]], axis=1)
+def steps_call(streams, slabs, cells, region, deriv_x, deriv_zt, filter_x, filter_zt):
+    _, rows, count, width, nz = cells.shape
+    nx = width * streams
     f32 = jnp.float32
     dma = pltpu.SemaphoreType.DMA
     return pl.pallas_call(
         functools.partial(steps_kernel, streams, slabs),
         out_shape=jax.ShapeDtypeStruct((streams, rows, count, nx // streams, nz), f32),
-        in_specs=[pl.BlockSpec(memory_space=pltpu.VMEM)] * 7,
+        in_specs=[pl.BlockSpec(memory_space=pltpu.VMEM)] * 6,
         out_specs=pl.BlockSpec(memory_space=pltpu.VMEM),
         scratch_shapes=[
             pltpu.VMEM((2, rows + 4, 2, nx, nz), f32),
@@ -446,13 +465,13 @@
             pltpu.VMEM((2, nx, nx), jnp.bfloat16),
             pltpu.VMEM((2, nz, nz), jnp.bfloat16),
             dma((2, 2)), dma((2, 2)), dma((2,)), dma((2,)), dma, dma,
-            dma((streams - 1, rows)), dma((streams - 1, rows)),
+            dma((streams - 1, rows)), dma((streams - 1, rows)), dma((streams - 1,)), dma((streams - 1,)),
             pltpu.SemaphoreType.REGULAR,
         ],
         compiler_params=pltpu.CompilerParams(
             collective_id=0, has_side_effects=True, vmem_limit_bytes=48 * 1024 * 1024
         ),
-    )(pv, uw, jnp.broadcast_to(region, (rows, nx, nz)), deriv_x, deriv_zt, filter_x, filter_zt)
+    )(cells, jnp.broadcast_to(region, (rows, nx, nz)), deriv_x, deriv_zt, filter_x, filter_zt)
 
 
 def plain_steps(order, fields, region, deriv_x, deriv_zt, filter_x, filter_zt):
@@ -492,10 +511,6 @@
     back = [streams - 1 - p for p in place]
 
     parts = fields.reshape(count, width_x, streams, rows, nz).transpose(2, 3, 0, 1, 4)
-    parts = jnp.where(even, jnp.stack([parts[p] for p in place]), jnp.stack([parts[p] for p in back]))
-    parts = lax.all_to_all(parts, "stream", split_axis=0, concat_axis=0, tiled=True)
-    fields = parts.transpose(1, 2, 0, 3, 4).reshape(rows, count, nx, nz)
-
     blocks = source_mask.astype(jnp.float32)
     region = jnp.repeat(jnp.repeat(blocks, MBLK, axis=0), MBLK, axis=1).T
     mine = jnp.asarray(place)[lax.axis_index("stream")]
@@ -505,8 +520,11 @@
 
     mats = (deriv_x, deriv_zt, filter_x, filter_zt)
     if rows >= 2:
-        parts = steps_call(streams, slabs, fields, region[:, 0], *mats)
+        parts = steps_call(streams, slabs, parts, region[:, 0], *mats)
         return parts.transpose(2, 3, 0, 1, 4).reshape(1, count, width_x, width_y, nz)
+    parts = jnp.where(even, jnp.stack([parts[p] for p in place]), jnp.stack([parts[p] for p in back]))
+    parts = lax.all_to_all(parts, "stream", split_axis=0, concat_axis=0, tiled=True)
+    fields = parts.transpose(1, 2, 0, 3, 4).reshape(rows, count, nx, nz)
     fields = plain_steps(order, fields, region, *mats)
 
     parts = fields.reshape(rows, count, streams, width_x, nz).transpose(2, 0, 1, 3, 4)

time: 157 us -> 153 us (0.975)
  Pallas kernels: 119 us -> 144 us
  waiting for transfers between devices: 24.6 us -> 0 us
  starting transfers between devices: 3.85 us -> 0 us
    pallas_call x1, Pallas kernels: 119 us -> 144 us  [steps_call(): pl.pallas_call(functools.partial(steps_kernel, streams, slabs), out_shape...]
    all_to_all x1 -> x0, waiting for transfers between devices: 24.6 us -> none  [shards(): lax.all_to_all(parts, 'stream', split_axis=0, concat_axis=0, tiled=True)]
    all_to_all x1 -> x0, starting transfers between devices: 3.85 us -> none  [shards(): lax.all_to_all(parts, 'stream', split_axis=0, concat_axis=0, tiled=True)]
    unnamed x13 -> x7, local copies, waits for them, and re-layouts: 3.17 us -> 4.2 us
  transfers between devices with their start and end apart: 1 -> 0, of which waited for: 1 -> 0; matrix products, arithmetic and copies ran while one was open for 0% -> 0% of each run, Pallas kernels for 0% -> 0%
where the time goes in v5:
time: 153 us; the launch traced here: 151 us
  Pallas kernels  144 us (94%)
  local copies, waits for them, and re-layouts  6.99 us (5%)
    pallas_call x1, Pallas kernels, steps_call(): pl.pallas_call(functools.partial(steps_kernel, streams, slabs), out_shape...  144 us
    unnamed x7, local copies, waits for them, and re-layouts  4.2 us

profile of v5, /device:TPU:16, one launch (start us, length us, event | category | flops | bytes accessed | tf_op | source)
XLA Modules:
  0.0 151.4 jit_solution(905466658888829154)
XLA Ops:
  0.0 0.7 convert_bitcast_fusion
  0.7 0.1 broadcast_in_dim.11
  0.7 0.1 broadcast_in_dim.12
  0.8 0.9 copy.8
  1.8 0.9 copy.9
  2.7 0.1 broadcast_in_dim.13.region_ref
  2.8 0.0 copy-start
  2.8 0.0 copy-start.1
  2.8 2.3 %copy.7 = f32[1,4,64,16,128]{4,2,1,3,0:T(8,128)S(1)} copy(f32[1,4,64,16,128]{4,3,2,1,0:T(8,128)} %param.6) | data formatting | bytes 4194304 | tf_op args[0]
  5.2 0.0 copy-done
  5.2 0.0 copy-done.1
  5.2 143.7 %shard_map.69 = f32[4,4,4,64,128]{4,3,2,1,0:T(8,128)S(1)} custom-call(f32[4,4,4,64,128]{4,3,2,1,0:T(8,128)S(1)} %bitcast.11, f32[4,256,128]{2,1,0:T(8,128)S(1)} %broadcast_in_dim.13.region_ref, f32[256,256]{1,0:T(8,128)S(1)} %copy-done, f32[128,128]{1,0:T(8,128)S(1)} %bitcast.12, f32[256,256]{1,0:T(8,128)S(1)} %copy-done.1, f32[128,128]{1,0:T(8,128)S(1)} %bitcast.13), custom_call_target="tpu_custom_call" | custom-call | tf_op jit(solution)/shard_map/pallas_call | solution.py:453
  148.9 2.5 %copy.10 = f32[1,4,64,16,128]{4,3,2,1,0:T(8,128)} copy(f32[1,4,64,16,128]{4,2,1,3,0:T(8,128)S(1)} %bitcast.10) | data formatting | bytes 4194304 | tf_op jit(solution)/shard_map/reshape | solution.py:524
Async XLA Ops:
  2.8 2.4 %copy-start = (f32[256,256]{1,0:T(8,128)S(1)}, f32[256,256]{1,0:T(8,128)}, u32[]{:S(2)}) copy-start(f32[256,256]{1,0:T(8,128)} %dx_ref.1) | copy-start | bytes 786436
  2.8 2.4 %copy-start.1 = (f32[256,256]{1,0:T(8,128)S(1)}, f32[256,256]{1,0:T(8,128)}, u32[]{:S(2)}) copy-start(f32[256,256]{1,0:T(8,128)} %fx_ref.1) | copy-start | bytes 786436
